TPU v7x, 512 devices: a whole 4x8x8 slice. The times are simulated.
512 devices in a mesh: row: 32 (over x_hi, y, core), frame: 16 (over z, x_lo).
Axes of the slice: x: 4 (x_hi: 2, x_lo: 2; x = x_hi * 2 + x_lo), y: 8, z: 8, core: 2. Of those that a mesh axis runs over, the one named last changes fastest.
Arguments:
- frames: bfloat16 [64, 64, 256, 128], P('frame', None, 'row'), may hold values from -6 to 6
- w_pair: bfloat16 [3, 3, 64, 128], replicated, may hold values from -0.1875 to 0.1875
- w_mixed: bfloat16 [3, 3, 64, 64], replicated, may hold values from -0.25 to 0.25
- slope_pair: float32 [64], replicated, may hold values from 0.05 to 0.5
- slope_mixed: float32 [64], replicated, may hold values from 0.05 to 0.5
Outputs:
- merged: bfloat16 [16, 64, 256, 128], P('frame', None, 'row')
All inputs are finite; a program needn't handle non-finite values.
Results may differ from a plain program's by a relative error of at most 0.0051.
Values may be sent and summed in bfloat16 or wider, within the bound.
No kernel may reach another device: no remote copies, remote signals or barrier semaphores. Data moves between devices by JAX's collectives and lax.ppermute only.
A program may use at most 64 MiB of HBM per device.

v0:
```python
import jax
import jax.numpy as jnp
from jax import lax
from jax.sharding import PartitionSpec as P


def padded_2(cells, sides, width):
    for axis, dim in sides:
        count = lax.axis_size(axis)
        ends = count - 1
        head = lax.slice_in_dim(cells, 0, width, axis=dim)
        tail = lax.slice_in_dim(cells, cells.shape[dim] - width, cells.shape[dim], axis=dim)
        cells = jnp.concatenate(
            [
                lax.ppermute(tail, axis, [(i, (i + 1) % count) for i in range(ends)]),
                cells,
                lax.ppermute(head, axis, [((i + 1) % count, i) for i in range(ends)]),
            ],
            axis=dim,
        )
    return cells


def swapped(block, axis, bit):
    count = lax.axis_size(axis)
    route = []
    for low in range(count):
        high = low | 1 << bit
        if high != low and high < count:
            route += [(low, high), (high, low)]
    return lax.ppermute(block, axis, route)


def prelu(values, slope):
    return jnp.where(values >= 0, values, slope[None, :, None, None] * values)


def convolve(padded, weight):
    out_rows = padded.shape[2] - 2
    cols = padded.shape[3]
    wide = jnp.pad(padded, ((0, 0), (0, 0), (0, 0), (1, 1)))
    total = jnp.zeros((padded.shape[0], weight.shape[2], out_rows, cols), jnp.float32)
    for tap_y in range(3):
        for tap_x in range(3):
            total = total + jnp.einsum(
                "oc,fchw->fohw",
                weight[tap_y, tap_x],
                wide[:, :, tap_y : tap_y + out_rows, tap_x : tap_x + cols],
                preferred_element_type=jnp.float32,
            )
    return total


def merge_block(first, second, w_pair, w_mixed, slope_pair, slope_mixed):
    joined = jnp.concatenate([first, second], axis=1)
    padded = padded_2(joined, (("row", 2),), 1)
    hidden = prelu(convolve(padded, w_pair), slope_pair).astype(jnp.bfloat16)
    padded_hidden = padded_2(hidden, (("row", 2),), 1)
    branch = prelu(convolve(padded_hidden, w_mixed), slope_mixed)
    return (first.astype(jnp.float32) + branch).astype(jnp.bfloat16)


def on_device(frames, w_pair, w_mixed, slope_pair, slope_mixed):
    count = lax.axis_size("frame")
    place = lax.axis_index("frame")
    top_bit = count.bit_length() - 2
    next_bit = top_bit - 1
    quarter = count // 4
    upper = place >= count // 2
    high = place // quarter % 2 == 1

    def merge(first, second):
        return merge_block(first, second, w_pair, w_mixed, slope_pair, slope_mixed)

    partner = swapped(frames, "frame", top_bit)
    level_one = merge(jnp.where(upper, partner, frames), jnp.where(upper, frames, partner))
    partner_one = swapped(level_one, "frame", next_bit)
    level_two = merge(
        jnp.where(high, partner_one, level_one), jnp.where(high, level_one, partner_one)
    )
    merged = lax.dynamic_slice_in_dim(level_two, place // quarter, 1, 0)
    return merged


def solution(mesh):
    placed = (P("frame", None, "row", None), P(), P(), P(), P())
    return jax.shard_map(
        on_device,
        mesh=mesh,
        in_specs=placed,
        out_specs=P("frame", None, "row", None),
        check_vma=False,
    )
```

profile of v0, /device:TPU:57, one launch (start us, length us, event | category | flops | bytes accessed | tf_op | source)
XLA Modules:
  0.0 127.6 jit_solution(10709827735184263587)
XLA Ops:
  0.0 1.2 copy.6
  1.2 10.6 %collective-permute-start = (bf16[4,64,8,128]{3,1,2,0:T(8,128)(2,1)S(1)}, bf16[4,64,8,128]{3,1,2,0:T(8,128)(2,1)S(1)}, u32[]{:S(2)}, u32[]{:S(2)}) collective-permute-start(bf16[4,64,8,128]{3,1,2,0:T(8,128)(2,1)S(1)} %copy.6), channel_id=1, source_target_pairs={{0,8},{8,0},{1,9},{9,1},{2,10},{10,2},{3,11},{11,3},{4,12},{12,4},... | collective-permute-start | bytes 1572872 | tf_op jit(solution)/shard_map/ppermute | solution.py:31
  11.9 11.7 %collective-permute-done = bf16[4,64,8,128]{3,1,2,0:T(8,128)(2,1)S(1)} collective-permute-done((bf16[4,64,8,128]{3,1,2,0:T(8,128)(2,1)S(1)}, bf16[4,64,8,128]{3,1,2,0:T(8,128)(2,1)S(1)}, u32[]{:S(2)}, u32[]{:S(2)}) %collective-permute-start) | collective-permute-done | bytes 524320 | tf_op jit(solution)/shard_map/ppermute | solution.py:31
  23.6 1.1 broadcast_select_fusion
  24.7 5.0 %collective-permute-start.1 = (bf16[4,128,1,128]{3,1,2,0:T(8,128)(2,1)S(1)}, bf16[4,128,1,128]{3,1,2,0:T(8,128)(2,1)S(1)}, u32[]{:S(2)}, u32[]{:S(2)}) collective-permute-start(bf16[4,128,1,128]{3,1,2,0:T(8,128)(2,1)S(1)} %get-tuple-element.9), channel_id=1, source_target_pairs={{0,16},{16,32},{32,48},{48,64},{64,80},{80,96},{96,112},{112,128},... | collective-permute-start | bytes 393224 | tf_op jit(solution)/shard_map/ppermute | solution.py:15
  29.8 1.9 %collective-permute-start.2 = (bf16[4,128,1,128]{3,1,2,0:T(8,128)(2,1)S(1)}, bf16[4,128,1,128]{3,1,2,0:T(8,128)(2,1)S(1)}, u32[]{:S(2)}, u32[]{:S(2)}) collective-permute-start(bf16[4,128,1,128]{3,1,2,0:T(8,128)(2,1)S(1)} %get-tuple-element.10), channel_id=1, source_target_pairs={{16,0},{32,16},{48,32},{64,48},{80,64},{96,80},{112,96},{128,112},... | collective-permute-start | bytes 393224 | tf_op jit(solution)/shard_map/ppermute | solution.py:17
  31.7 0.3 fusion.58
  32.0 7.7 %collective-permute-done.2 = bf16[4,128,1,128]{3,1,2,0:T(8,128)(2,1)S(1)} collective-permute-done((bf16[4,128,1,128]{3,1,2,0:T(8,128)(2,1)S(1)}, bf16[4,128,1,128]{3,1,2,0:T(8,128)(2,1)S(1)}, u32[]{:S(2)}, u32[]{:S(2)}) %collective-permute-start.2) | collective-permute-done | bytes 131104 | tf_op jit(solution)/shard_map/ppermute | solution.py:17
  39.7 2.2 %select_maximum_fusion.3 = bf16[4,128,10,130]{3,1,2,0:T(8,128)(2,1)S(1)} fusion(bf16[4,128,1,128]{3,1,2,0:T(8,128)(2,1)S(1)} %collective-permute-done.2, bf16[4,128,1,128]{3,1,2,0:T(8,128)(2,1)S(1)} %collective-permute-done.1, bf16[4,64,8,128]{3,1,2,0:T(8,128)(2,1)S(1)} %get-tuple-element.11, bf16[4,64,8,128]{3,1,2,0:T(8,128)(2,1)S(1)} %get-tuple-element.12), kind=kLoop, calls=%fused_computation.11 | loop fusion | flops 9984000 | bytes 2641920 | tf_op jit(solution)/shard_map/concatenate | solution.py:13
  41.9 0.3 fusion.47
  42.2 0.6 fusion.49
  42.7 0.3 fusion.51
  43.0 0.6 fusion.53
  43.6 0.6 fusion.43
  44.2 0.3 fusion.45
  44.5 0.3 fusion.55
  44.8 0.0 copy-done.2
  44.8 0.7 fusion.26
  45.6 1.9 %collective-permute-start.3 = (bf16[4,64,1,128]{3,1,2,0:T(8,128)(2,1)S(1)}, bf16[4,64,1,128]{3,1,2,0:T(8,128)(2,1)S(1)}, u32[]{:S(2)}, u32[]{:S(2)}) collective-permute-start(bf16[4,64,1,128]{3,1,2,0:T(8,128)(2,1)S(1)} %get-tuple-element.15), channel_id=1, source_target_pairs={{0,16},{16,32},{32,48},{48,64},{64,80},{80,96},{96,112},{112,128},... | collective-permute-start | bytes 196616 | tf_op jit(solution)/shard_map/ppermute | solution.py:15
  47.5 2.4 %collective-permute-start.4 = (bf16[4,64,1,128]{3,1,2,0:T(8,128)(2,1)S(1)}, bf16[4,64,1,128]{3,1,2,0:T(8,128)(2,1)S(1)}, u32[]{:S(2)}, u32[]{:S(2)}) collective-permute-start(bf16[4,64,1,128]{3,1,2,0:T(8,128)(2,1)S(1)} %get-tuple-element.16), channel_id=1, source_target_pairs={{16,0},{32,16},{48,32},{64,48},{80,64},{96,80},{112,96},{128,112},... | collective-permute-start | bytes 196616 | tf_op jit(solution)/shard_map/ppermute | solution.py:17
  49.9 0.0 collective-permute-done.3
  49.9 6.8 %collective-permute-done.4 = bf16[4,64,1,128]{3,1,2,0:T(8,128)(2,1)S(1)} collective-permute-done((bf16[4,64,1,128]{3,1,2,0:T(8,128)(2,1)S(1)}, bf16[4,64,1,128]{3,1,2,0:T(8,128)(2,1)S(1)}, u32[]{:S(2)}, u32[]{:S(2)}) %collective-permute-start.4) | collective-permute-done | bytes 65568 | tf_op jit(solution)/shard_map/ppermute | solution.py:17
  56.7 0.7 select_maximum_fusion.7
  57.4 0.4 fusion.76
  57.8 0.3 fusion.83
  58.1 0.3 convolution_add_fusion.15
  58.3 0.4 convolution_add_fusion.14
  58.7 0.3 convolution_add_fusion.13
  59.0 0.3 convolution_add_fusion.12
  59.3 0.0 copy-start.3
  59.3 0.4 convolution_add_fusion.11
  59.7 0.3 convolution_add_fusion.10
  60.0 0.4 add_convert_fusion
  60.4 15.2 %collective-permute-start.5 = (bf16[4,64,8,128]{3,1,2,0:T(8,128)(2,1)S(1)}, bf16[4,64,8,128]{3,1,2,0:T(8,128)(2,1)S(1)}, u32[]{:S(2)}, u32[]{:S(2)}) collective-permute-start(bf16[4,64,8,128]{3,1,2,0:T(8,128)(2,1)S(1)} %add_convert_fusion), channel_id=1, source_target_pairs={{0,4},{4,0},{1,5},{5,1},{2,6},{6,2},{3,7},{7,3},{8,12},{12,8},{9,1... | collective-permute-start | bytes 1572872 | tf_op jit(solution)/shard_map/ppermute | solution.py:31
  75.6 18.7 %collective-permute-done.5 = bf16[4,64,8,128]{3,1,2,0:T(8,128)(2,1)S(1)} collective-permute-done((bf16[4,64,8,128]{3,1,2,0:T(8,128)(2,1)S(1)}, bf16[4,64,8,128]{3,1,2,0:T(8,128)(2,1)S(1)}, u32[]{:S(2)}, u32[]{:S(2)}) %collective-permute-start.5) | collective-permute-done | bytes 524320 | tf_op jit(solution)/shard_map/ppermute | solution.py:31
  94.3 0.1 broadcast_select_fusion.3
  94.4 1.9 %collective-permute-start.6 = (bf16[4,128,1,128]{3,1,2,0:T(8,128)(2,1)S(1)}, bf16[4,128,1,128]{3,1,2,0:T(8,128)(2,1)S(1)}, u32[]{:S(2)}, u32[]{:S(2)}) collective-permute-start(bf16[4,128,1,128]{3,1,2,0:T(8,128)(2,1)S(1)} %get-tuple-element.5), channel_id=1, source_target_pairs={{0,16},{16,32},{32,48},{48,64},{64,80},{80,96},{96,112},{112,128},... | collective-permute-start | bytes 393224 | tf_op jit(solution)/shard_map/ppermute | solution.py:15
  96.3 2.6 %collective-permute-start.7 = (bf16[4,128,1,128]{3,1,2,0:T(8,128)(2,1)S(1)}, bf16[4,128,1,128]{3,1,2,0:T(8,128)(2,1)S(1)}, u32[]{:S(2)}, u32[]{:S(2)}) collective-permute-start(bf16[4,128,1,128]{3,1,2,0:T(8,128)(2,1)S(1)} %get-tuple-element.6), channel_id=1, source_target_pairs={{16,0},{32,16},{48,32},{64,48},{80,64},{96,80},{112,96},{128,112},... | collective-permute-start | bytes 393224 | tf_op jit(solution)/shard_map/ppermute | solution.py:17
  98.9 0.3 fusion.62
  99.2 7.0 %collective-permute-done.7 = bf16[4,128,1,128]{3,1,2,0:T(8,128)(2,1)S(1)} collective-permute-done((bf16[4,128,1,128]{3,1,2,0:T(8,128)(2,1)S(1)}, bf16[4,128,1,128]{3,1,2,0:T(8,128)(2,1)S(1)}, u32[]{:S(2)}, u32[]{:S(2)}) %collective-permute-start.7) | collective-permute-done | bytes 131104 | tf_op jit(solution)/shard_map/ppermute | solution.py:17
  106.2 2.2 %select_maximum_fusion = bf16[4,128,10,130]{3,1,2,0:T(8,128)(2,1)S(1)} fusion(bf16[4,128,1,128]{3,1,2,0:T(8,128)(2,1)S(1)} %collective-permute-done.7, bf16[4,128,1,128]{3,1,2,0:T(8,128)(2,1)S(1)} %collective-permute-done.6, bf16[4,64,8,128]{3,1,2,0:T(8,128)(2,1)S(1)} %get-tuple-element.8, bf16[4,64,8,128]{3,1,2,0:T(8,128)(2,1)S(1)} %get-tuple-element.7), kind=kLoop, calls=%fused_computation.8 | loop fusion | flops 9984000 | bytes 2641920 | tf_op jit(solution)/shard_map/concatenate | solution.py:13
  108.4 0.3 fusion.32
  108.7 0.6 fusion.34
  109.3 0.3 fusion.36
  109.6 0.6 fusion.38
  110.1 0.6 fusion.28
  110.7 0.3 fusion.30
  111.0 0.3 fusion.40
  111.3 0.7 fusion.27
  112.1 1.9 %collective-permute-start.8 = (bf16[4,64,1,128]{3,1,2,0:T(8,128)(2,1)S(1)}, bf16[4,64,1,128]{3,1,2,0:T(8,128)(2,1)S(1)}, u32[]{:S(2)}, u32[]{:S(2)}) collective-permute-start(bf16[4,64,1,128]{3,1,2,0:T(8,128)(2,1)S(1)} %get-tuple-element.13), channel_id=1, source_target_pairs={{0,16},{16,32},{32,48},{48,64},{64,80},{80,96},{96,112},{112,128},... | collective-permute-start | bytes 196616 | tf_op jit(solution)/shard_map/ppermute | solution.py:15
  114.0 2.4 %collective-permute-start.9 = (bf16[4,64,1,128]{3,1,2,0:T(8,128)(2,1)S(1)}, bf16[4,64,1,128]{3,1,2,0:T(8,128)(2,1)S(1)}, u32[]{:S(2)}, u32[]{:S(2)}) collective-permute-start(bf16[4,64,1,128]{3,1,2,0:T(8,128)(2,1)S(1)} %get-tuple-element.14), channel_id=1, source_target_pairs={{16,0},{32,16},{48,32},{64,48},{80,64},{96,80},{112,96},{128,112},... | collective-permute-start | bytes 196616 | tf_op jit(solution)/shard_map/ppermute | solution.py:17
  116.4 6.8 %collective-permute-done.9 = bf16[4,64,1,128]{3,1,2,0:T(8,128)(2,1)S(1)} collective-permute-done((bf16[4,64,1,128]{3,1,2,0:T(8,128)(2,1)S(1)}, bf16[4,64,1,128]{3,1,2,0:T(8,128)(2,1)S(1)}, u32[]{:S(2)}, u32[]{:S(2)}) %collective-permute-start.9) | collective-permute-done | bytes 65568 | tf_op jit(solution)/shard_map/ppermute | solution.py:17
  123.2 0.7 select_maximum_fusion.5
  123.9 0.4 fusion.66
  124.3 0.3 fusion.73
  124.5 0.3 convolution_add_fusion.8
  124.8 0.4 convolution_add_fusion.7
  125.2 0.3 convolution_add_fusion.6
  125.5 0.3 convolution_add_fusion.5
  125.8 0.4 convolution_add_fusion.4
  126.1 0.3 convolution_add_fusion.3
  126.4 0.3 fusion.16
  126.7 0.1 fusion.87
  126.8 0.7 copy.9
  (13 shorter events, 0.1 us)
Async XLA Ops:
  0.0 31.7 %copy-start.1 = (bf16[3,3,64,128]{3,2,1,0:T(8,128)(2,1)S(1)}, bf16[3,3,64,128]{3,2,1,0:T(8,128)(2,1)}, u32[]{:S(2)}) copy-start(bf16[3,3,64,128]{3,2,1,0:T(8,128)(2,1)} %param.6) | copy-start | bytes 442372
  1.2 22.4 %collective-permute-start = (bf16[4,64,8,128]{3,1,2,0:T(8,128)(2,1)S(1)}, bf16[4,64,8,128]{3,1,2,0:T(8,128)(2,1)S(1)}, u32[]{:S(2)}, u32[]{:S(2)}) collective-permute-start(bf16[4,64,8,128]{3,1,2,0:T(8,128)(2,1)S(1)} %copy.6), channel_id=1, source_target_pairs={{0,8},{8,0},{1,9},{9,1},{2,10},{10,2},{3,11},{11,3},{4,12},{12,4},... | collective-permute-start | bytes 1572872 | tf_op jit(solution)/shard_map/ppermute | solution.py:31
  24.7 7.3 %collective-permute-start.1 = (bf16[4,128,1,128]{3,1,2,0:T(8,128)(2,1)S(1)}, bf16[4,128,1,128]{3,1,2,0:T(8,128)(2,1)S(1)}, u32[]{:S(2)}, u32[]{:S(2)}) collective-permute-start(bf16[4,128,1,128]{3,1,2,0:T(8,128)(2,1)S(1)} %get-tuple-element.9), channel_id=1, source_target_pairs={{0,16},{16,32},{32,48},{48,64},{64,80},{80,96},{96,112},{112,128},... | collective-permute-start | bytes 393224 | tf_op jit(solution)/shard_map/ppermute | solution.py:15
  29.8 9.9 %collective-permute-start.2 = (bf16[4,128,1,128]{3,1,2,0:T(8,128)(2,1)S(1)}, bf16[4,128,1,128]{3,1,2,0:T(8,128)(2,1)S(1)}, u32[]{:S(2)}, u32[]{:S(2)}) collective-permute-start(bf16[4,128,1,128]{3,1,2,0:T(8,128)(2,1)S(1)} %get-tuple-element.10), channel_id=1, source_target_pairs={{16,0},{32,16},{48,32},{64,48},{80,64},{96,80},{112,96},{128,112},... | collective-permute-start | bytes 393224 | tf_op jit(solution)/shard_map/ppermute | solution.py:17
  44.1 0.7 copy-start.2
  44.8 12.6 %copy-start = (bf16[3,3,64,64]{3,2,1,0:T(8,128)(2,1)S(1)}, bf16[3,3,64,64]{3,2,1,0:T(8,128)(2,1)}, u32[]{:S(2)}) copy-start(bf16[3,3,64,64]{3,2,1,0:T(8,128)(2,1)} %param.7) | copy-start | bytes 221188
  45.6 4.3 %collective-permute-start.3 = (bf16[4,64,1,128]{3,1,2,0:T(8,128)(2,1)S(1)}, bf16[4,64,1,128]{3,1,2,0:T(8,128)(2,1)S(1)}, u32[]{:S(2)}, u32[]{:S(2)}) collective-permute-start(bf16[4,64,1,128]{3,1,2,0:T(8,128)(2,1)S(1)} %get-tuple-element.15), channel_id=1, source_target_pairs={{0,16},{16,32},{32,48},{48,64},{64,80},{80,96},{96,112},{112,128},... | collective-permute-start | bytes 196616 | tf_op jit(solution)/shard_map/ppermute | solution.py:15
  47.5 9.2 %collective-permute-start.4 = (bf16[4,64,1,128]{3,1,2,0:T(8,128)(2,1)S(1)}, bf16[4,64,1,128]{3,1,2,0:T(8,128)(2,1)S(1)}, u32[]{:S(2)}, u32[]{:S(2)}) collective-permute-start(bf16[4,64,1,128]{3,1,2,0:T(8,128)(2,1)S(1)} %get-tuple-element.16), channel_id=1, source_target_pairs={{16,0},{32,16},{48,32},{64,48},{80,64},{96,80},{112,96},{128,112},... | collective-permute-start | bytes 196616 | tf_op jit(solution)/shard_map/ppermute | solution.py:17
  59.3 0.7 copy-start.3
  60.4 33.9 %collective-permute-start.5 = (bf16[4,64,8,128]{3,1,2,0:T(8,128)(2,1)S(1)}, bf16[4,64,8,128]{3,1,2,0:T(8,128)(2,1)S(1)}, u32[]{:S(2)}, u32[]{:S(2)}) collective-permute-start(bf16[4,64,8,128]{3,1,2,0:T(8,128)(2,1)S(1)} %add_convert_fusion), channel_id=1, source_target_pairs={{0,4},{4,0},{1,5},{5,1},{2,6},{6,2},{3,7},{7,3},{8,12},{12,8},{9,1... | collective-permute-start | bytes 1572872 | tf_op jit(solution)/shard_map/ppermute | solution.py:31
  94.4 4.8 %collective-permute-start.6 = (bf16[4,128,1,128]{3,1,2,0:T(8,128)(2,1)S(1)}, bf16[4,128,1,128]{3,1,2,0:T(8,128)(2,1)S(1)}, u32[]{:S(2)}, u32[]{:S(2)}) collective-permute-start(bf16[4,128,1,128]{3,1,2,0:T(8,128)(2,1)S(1)} %get-tuple-element.5), channel_id=1, source_target_pairs={{0,16},{16,32},{32,48},{48,64},{64,80},{80,96},{96,112},{112,128},... | collective-permute-start | bytes 393224 | tf_op jit(solution)/shard_map/ppermute | solution.py:15
  96.3 9.9 %collective-permute-start.7 = (bf16[4,128,1,128]{3,1,2,0:T(8,128)(2,1)S(1)}, bf16[4,128,1,128]{3,1,2,0:T(8,128)(2,1)S(1)}, u32[]{:S(2)}, u32[]{:S(2)}) collective-permute-start(bf16[4,128,1,128]{3,1,2,0:T(8,128)(2,1)S(1)} %get-tuple-element.6), channel_id=1, source_target_pairs={{16,0},{32,16},{48,32},{64,48},{80,64},{96,80},{112,96},{128,112},... | collective-permute-start | bytes 393224 | tf_op jit(solution)/shard_map/ppermute | solution.py:17
  112.1 4.4 %collective-permute-start.8 = (bf16[4,64,1,128]{3,1,2,0:T(8,128)(2,1)S(1)}, bf16[4,64,1,128]{3,1,2,0:T(8,128)(2,1)S(1)}, u32[]{:S(2)}, u32[]{:S(2)}) collective-permute-start(bf16[4,64,1,128]{3,1,2,0:T(8,128)(2,1)S(1)} %get-tuple-element.13), channel_id=1, source_target_pairs={{0,16},{16,32},{32,48},{48,64},{64,80},{80,96},{96,112},{112,128},... | collective-permute-start | bytes 196616 | tf_op jit(solution)/shard_map/ppermute | solution.py:15
  114.0 9.2 %collective-permute-start.9 = (bf16[4,64,1,128]{3,1,2,0:T(8,128)(2,1)S(1)}, bf16[4,64,1,128]{3,1,2,0:T(8,128)(2,1)S(1)}, u32[]{:S(2)}, u32[]{:S(2)}) collective-permute-start(bf16[4,64,1,128]{3,1,2,0:T(8,128)(2,1)S(1)} %get-tuple-element.14), channel_id=1, source_target_pairs={{16,0},{32,16},{48,32},{64,48},{80,64},{96,80},{112,96},{128,112},... | collective-permute-start | bytes 196616 | tf_op jit(solution)/shard_map/ppermute | solution.py:17
where the time goes:
time: 128 us
  waiting for transfers between devices  58.6 us (46%)
  starting transfers between devices  45.9 us (36%)
  matrix products  13.5 us (11%)
  other arithmetic  7.09 us (6%)
  local copies, waits for them, and re-layouts  2.02 us (2%)
    ppermute x2, waiting for transfers between devices, swapped(): return lax.ppermute(block, axis, route)  30.4 us
    ppermute x4, waiting for transfers between devices, padded_2(): lax.ppermute(head, axis, [((i + 1) % count, i) for i in range(ends)])  28.2 us
    ppermute x2, starting transfers between devices, swapped(): return lax.ppermute(block, axis, route)  25.8 us
    dot_general x36, matrix products, convolve(): jnp.einsum('oc,fchw->fohw', weight[tap_y, tap_x], wide[:, :, tap_y:tap_y...  13.5 us
    ppermute x4, starting transfers between devices, padded_2(): lax.ppermute(tail, axis, [(i, (i + 1) % count) for i in range(ends)])  10.8 us
    ppermute x4, starting transfers between devices, padded_2(): lax.ppermute(head, axis, [((i + 1) % count, i) for i in range(ends)])  9.32 us
    concatenate x4, other arithmetic, padded_2(): jnp.concatenate([lax.ppermute(tail, axis, [(i, (i + 1) % count) for i in...  5.73 us
  transfers between devices with their start and end apart: 10, of which 6 were waited for; matrix products, arithmetic and copies ran while one was open for 0% of the time, Pallas kernels for 0%

commit v1 on v0

v1 whole, which is shorter than its diff:
```python
import jax
import jax.numpy as jnp
from jax import lax
from jax.experimental import pallas as pl
from jax.experimental.pallas import tpu as pltpu
from jax.sharding import PartitionSpec as P

ROWS = 8
HALO = 4
CH = 64
LANES = 128


def rows_first(stack):
    def body(src, top, bottom, wide):
        for slot, frame in enumerate((0, 2, 1, 3)):
            wide[...] = src[frame].astype(jnp.float32).reshape(CH * ROWS, LANES)
            for row in range(ROWS):
                value = wide[pl.ds(row, CH, stride=ROWS), :].astype(jnp.bfloat16)
                half = top if row < HALO else bottom
                half[row % HALO, slot * CH : (slot + 1) * CH, :] = value

    half = jax.ShapeDtypeStruct((HALO, 4 * CH, LANES), jnp.bfloat16)
    return pl.pallas_call(
        body,
        out_shape=(half, half),
        scratch_shapes=[pltpu.VMEM((CH * ROWS, LANES), jnp.float32)],
        name="rows_first",
    )(stack)


def merges(above, top, bottom, below, w_pair, w_mixed, slope_pair, slope_mixed):
    def body(above_r, top_r, bottom_r, below_r, wp_r, wm_r, sp_r, sm_r, out_r, hid, one, wide):
        place = lax.axis_index("row")
        last = lax.axis_size("row") - 1
        lane = lax.broadcasted_iota(jnp.int32, (CH, LANES), 1)
        not_first = lane > 0
        not_last = lane < LANES - 1
        square = lax.broadcasted_iota(jnp.int32, (CH, CH), 0) == lax.broadcasted_iota(jnp.int32, (CH, CH), 1)

        def column(slope):
            return jnp.sum(jnp.where(square, slope[...], 0.0), axis=1, keepdims=True)

        s_pair = column(sp_r)
        s_mixed = column(sm_r)
        lhs_pair = jnp.concatenate([wp_r[0], wp_r[1], wp_r[2]], axis=1)
        lhs_mixed = jnp.concatenate([wm_r[0], wm_r[1], wm_r[2]], axis=1)
        halves = (above_r, top_r, bottom_r, below_r)

        def frame_row(row, pair):
            return halves[row // HALO][row % HALO, pair * 2 * CH : (pair + 1) * 2 * CH, :]

        def inside(row, value):
            if row < HALO:
                return jnp.where(place > 0, value, 0.0)
            if row >= HALO + ROWS:
                return jnp.where(place < last, value, 0.0)
            return value

        def fold(part, slope):
            left = jnp.where(not_first, pltpu.roll(part[:CH], 1, 1), 0.0)
            right = jnp.where(not_last, pltpu.roll(part[2 * CH :], LANES - 1, 1), 0.0)
            total = part[CH : 2 * CH] + left + right
            return jnp.where(total >= 0, total, slope * total)

        def level(load, base, low, high, emit):
            for row in range(low - 1, high + 1, 2):
                rows = [load(r) for r in range(row - 1, row + 3)]
                rhs = jnp.concatenate(
                    [jnp.concatenate(rows[0:3], axis=0), jnp.concatenate(rows[1:4], axis=0)], axis=1
                )
                both = jnp.dot(lhs_pair, rhs, preferred_element_type=jnp.float32)
                for k in range(2):
                    value = fold(both[:, k * LANES : (k + 1) * LANES], s_pair)
                    hid[base + row + k] = inside(row + k, value).astype(jnp.bfloat16)
            for row in range(low, high, 2):
                rows = [hid[base + r] for r in range(row - 1, row + 3)]
                rhs = jnp.concatenate(
                    [jnp.concatenate(rows[0:3], axis=0), jnp.concatenate(rows[1:4], axis=0)], axis=1
                )
                both = jnp.dot(lhs_mixed, rhs, preferred_element_type=jnp.float32)
                for k in range(2):
                    emit(row + k, fold(both[:, k * LANES : (k + 1) * LANES], s_mixed))

        for pair in range(2):

            def emit_one(row, branch, pair=pair):
                first = frame_row(row, pair)[:CH].astype(jnp.float32)
                one[row, pair * CH : (pair + 1) * CH, :] = inside(row, first + branch).astype(jnp.bfloat16)

            level(lambda row, pair=pair: frame_row(row, pair), 16 * pair, 2, 14, emit_one)

        def emit_two(row, branch):
            first = one[row, :CH, :].astype(jnp.float32)
            wide[pl.ds(row - HALO, CH, stride=ROWS), :] = first + branch

        level(lambda row: one[row], 32, HALO, HALO + ROWS, emit_two)
        out_r[...] = wide[...].reshape(CH, ROWS, LANES).astype(jnp.bfloat16)

    return pl.pallas_call(
        body,
        out_shape=jax.ShapeDtypeStruct((CH, ROWS, LANES), jnp.bfloat16),
        scratch_shapes=[
            pltpu.VMEM((48, CH, LANES), jnp.bfloat16),
            pltpu.VMEM((16, 2 * CH, LANES), jnp.bfloat16),
            pltpu.VMEM((CH * ROWS, LANES), jnp.float32),
        ],
        name="merges",
    )(above, top, bottom, below, w_pair, w_mixed, slope_pair, slope_mixed)


def on_device(frames, w_pair, w_mixed, slope_pair, slope_mixed):
    count = lax.axis_size("frame")
    quarter = count // 4
    groups = [[a + quarter * b for b in range(4)] for a in range(quarter)]
    stack = lax.all_to_all(frames, "frame", 0, 0, axis_index_groups=groups, tiled=True)
    top, bottom = rows_first(stack)
    ends = lax.axis_size("row") - 1
    above = lax.ppermute(bottom, "row", [(i, i + 1) for i in range(ends)])
    below = lax.ppermute(top, "row", [(i + 1, i) for i in range(ends)])
    merged = merges(
        above,
        top,
        bottom,
        below,
        w_pair.reshape(3, 3 * CH, 2 * CH),
        w_mixed.reshape(3, 3 * CH, CH),
        slope_pair.reshape(1, CH),
        slope_mixed.reshape(1, CH),
    )
    return merged[None]


def solution(mesh):
    placed = (P("frame", None, "row", None), P(), P(), P(), P())
    return jax.shard_map(
        on_device,
        mesh=mesh,
        in_specs=placed,
        out_specs=P("frame", None, "row", None),
        check_vma=False,
    )
```

time: 128 us -> 50.6 us (0.40)
  waiting for transfers between devices: 58.6 us -> 9.58 us
  starting transfers between devices: 45.9 us -> 10.2 us
  blocking collectives: 0 us -> 23.5 us
  matrix products: 13.5 us -> 0 us
  other arithmetic: 7.09 us -> 0 us
  Pallas kernels: 0 us -> 6.32 us
  local copies, waits for them, and re-layouts: 2.02 us -> 0.7 us
    ppermute x10 -> x2, waiting for transfers between devices: 58.6 us -> 9.58 us  [the longest x1 7.9 us: on_device(): below = lax.ppermute(top, 'row', [(i + 1, i) for i in range(ends)])]
    ppermute x10 -> x2, starting transfers between devices: 45.9 us -> 10.2 us  [the longest x1 8.29 us: on_device(): above = lax.ppermute(bottom, 'row', [(i, i + 1) for i in range(ends)])]
    all_to_all x0 -> x1, blocking collectives: none -> 23.5 us  [on_device(): lax.all_to_all(frames, 'frame', 0, 0, axis_index_groups=groups, tiled=True)]
    dot_general x36 -> x0, matrix products: 13.5 us -> none  [convolve(): jnp.einsum('oc,fchw->fohw', weight[tap_y, tap_x], wide[:, :, tap_y:tap_y...]
    pallas_call x0 -> x2, Pallas kernels: none -> 6.32 us  [the longest x1 4.27 us: merges(): pl.pallas_call(body, out_shape=jax.ShapeDtypeStruct((CH, ROWS, LANES), jn...]
    concatenate x4 -> x0, other arithmetic: 5.73 us -> none  [padded_2(): jnp.concatenate([lax.ppermute(tail, axis, [(i, (i + 1) % count) for i in...]
  transfers between devices with their start and end apart: 10 -> 2, of which waited for: 6 -> 2; matrix products, arithmetic and copies ran while one was open for 0% -> 0% of each run, Pallas kernels for 0% -> 0%
where the time goes in v1:
time: 50.6 us; the launch traced here: 50.3 us
  blocking collectives  23.5 us (46%)
  starting transfers between devices  10.2 us (20%)
  waiting for transfers between devices  9.58 us (19%)
  Pallas kernels  6.32 us (12%)
  local copies, waits for them, and re-layouts  0.7 us (1%)
    all_to_all x1, blocking collectives, on_device(): lax.all_to_all(frames, 'frame', 0, 0, axis_index_groups=groups, tiled=True)  23.5 us
    ppermute x1, starting transfers between devices, on_device(): above = lax.ppermute(bottom, 'row', [(i, i + 1) for i in range(ends)])  8.29 us
    ppermute x1, waiting for transfers between devices, on_device(): below = lax.ppermute(top, 'row', [(i + 1, i) for i in range(ends)])  7.9 us
    pallas_call x1, Pallas kernels, merges(): pl.pallas_call(body, out_shape=jax.ShapeDtypeStruct((CH, ROWS, LANES), jn...  4.27 us
    pallas_call x1, Pallas kernels, rows_first(): pl.pallas_call(body, out_shape=(half, half), scratch_shapes=[pltpu.VMEM((...  2.05 us
    ppermute x1, starting transfers between devices, on_device(): below = lax.ppermute(top, 'row', [(i + 1, i) for i in range(ends)])  1.92 us
    ppermute x1, waiting for transfers between devices, on_device(): above = lax.ppermute(bottom, 'row', [(i, i + 1) for i in range(ends)])  1.68 us
  transfers between devices with their start and end apart: 2, of which 2 were waited for; matrix products, arithmetic and copies ran while one was open for 0% of the time, Pallas kernels for 0%

profile of v1, /device:TPU:57, one launch (start us, length us, event | category | flops | bytes accessed | tf_op | source)
XLA Modules:
  0.0 50.3 jit_solution(12548371884861411851)
XLA Ops:
  0.0 23.5 %all_to_all.5.src = bf16[4,64,8,128]{3,2,1,0:T(8,128)(2,1)} all-to-all(bf16[4,64,8,128]{3,2,1,0:T(8,128)(2,1)} %param.5), channel_id=1, replica_groups={{0,4,8,12},{1,5,9,13},{2,6,10,14},{3,7,11,15},{16,20,24,28},{17,21,25,2..., dimensions={0} | all-to-all | bytes 1048576 | tf_op jit(solution)/shard_map/all_to_all | solution.py:116
  23.5 2.1 %rows_first.1 = (bf16[4,256,128]{2,1,0:T(8,128)(2,1)}, bf16[4,256,128]{2,1,0:T(8,128)(2,1)}) custom-call(bf16[4,64,8,128]{3,2,1,0:T(8,128)(2,1)} %all_to_all.5.src), custom_call_target="tpu_custom_call" | custom-call | tf_op jit(solution)/shard_map/rows_first/pallas_call | solution.py:24
  25.5 8.3 %collective-permute-start = (bf16[4,256,128]{2,1,0:T(8,128)(2,1)}, bf16[4,256,128]{2,1,0:T(8,128)(2,1)S(1)}, u32[]{:S(2)}, u32[]{:S(2)}) collective-permute-start(bf16[4,256,128]{2,1,0:T(8,128)(2,1)} %get-tuple-element.7.bottom_r), channel_id=1, source_target_pairs={{0,16},{16,32},{32,48},{48,64},{64,80},{80,96},{96,112},{112,128},... | collective-permute-start | bytes 786440 | tf_op jit(solution)/shard_map/ppermute | solution.py:119
  33.8 1.9 %collective-permute-start.1 = (bf16[4,256,128]{2,1,0:T(8,128)(2,1)}, bf16[4,256,128]{2,1,0:T(8,128)(2,1)S(1)}, u32[]{:S(2)}, u32[]{:S(2)}) collective-permute-start(bf16[4,256,128]{2,1,0:T(8,128)(2,1)} %get-tuple-element.8.top_r), channel_id=1, source_target_pairs={{16,0},{32,16},{48,32},{64,48},{80,64},{96,80},{112,96},{128,112},... | collective-permute-start | bytes 786440 | tf_op jit(solution)/shard_map/ppermute | solution.py:120
  35.7 1.7 %collective-permute-done.above_r = bf16[4,256,128]{2,1,0:T(8,128)(2,1)S(1)} collective-permute-done((bf16[4,256,128]{2,1,0:T(8,128)(2,1)}, bf16[4,256,128]{2,1,0:T(8,128)(2,1)S(1)}, u32[]{:S(2)}, u32[]{:S(2)}) %collective-permute-start) | collective-permute-done | bytes 262176 | tf_op jit(solution)/shard_map/ppermute | solution.py:119
  37.4 0.0 copy-start
  37.4 7.9 %collective-permute-done.1.below_r = bf16[4,256,128]{2,1,0:T(8,128)(2,1)S(1)} collective-permute-done((bf16[4,256,128]{2,1,0:T(8,128)(2,1)}, bf16[4,256,128]{2,1,0:T(8,128)(2,1)S(1)}, u32[]{:S(2)}, u32[]{:S(2)}) %collective-permute-start.1) | collective-permute-done | bytes 262176 | tf_op jit(solution)/shard_map/ppermute | solution.py:120
  45.3 0.0 copy-start.1
  45.3 0.0 copy-done
  45.3 0.7 %copy-done.1 = bf16[4,256,128]{2,1,0:T(8,128)(2,1)} copy-done((bf16[4,256,128]{2,1,0:T(8,128)(2,1)}, bf16[4,256,128]{2,1,0:T(8,128)(2,1)S(1)}, u32[]{:S(2)}) %copy-start.1) | copy-done | bytes 262168
  46.0 4.3 %merges.1 = bf16[64,8,128]{2,1,0:T(8,128)(2,1)} custom-call(bf16[4,256,128]{2,1,0:T(8,128)(2,1)} %copy-done, bf16[4,256,128]{2,1,0:T(8,128)(2,1)} %get-tuple-element.8.top_r, bf16[4,256,128]{2,1,0:T(8,128)(2,1)} %get-tuple-element.7.bottom_r, bf16[4,256,128]{2,1,0:T(8,128)(2,1)} %copy-done.1, bf16[3,192,128]{2,1,0:T(8,128)(2,1)} %bitcast.5, ...), custom_call_target="tpu_custom_call" | custom-call | tf_op jit(solution)/shard_map/merges/pallas_call | solution.py:100
Async XLA Ops:
  25.5 11.9 %collective-permute-start = (bf16[4,256,128]{2,1,0:T(8,128)(2,1)}, bf16[4,256,128]{2,1,0:T(8,128)(2,1)S(1)}, u32[]{:S(2)}, u32[]{:S(2)}) collective-permute-start(bf16[4,256,128]{2,1,0:T(8,128)(2,1)} %get-tuple-element.7.bottom_r), channel_id=1, source_target_pairs={{0,16},{16,32},{32,48},{48,64},{64,80},{80,96},{96,112},{112,128},... | collective-permute-start | bytes 786440 | tf_op jit(solution)/shard_map/ppermute | solution.py:119
  33.8 11.5 %collective-permute-start.1 = (bf16[4,256,128]{2,1,0:T(8,128)(2,1)}, bf16[4,256,128]{2,1,0:T(8,128)(2,1)S(1)}, u32[]{:S(2)}, u32[]{:S(2)}) collective-permute-start(bf16[4,256,128]{2,1,0:T(8,128)(2,1)} %get-tuple-element.8.top_r), channel_id=1, source_target_pairs={{16,0},{32,16},{48,32},{64,48},{80,64},{96,80},{112,96},{128,112},... | collective-permute-start | bytes 786440 | tf_op jit(solution)/shard_map/ppermute | solution.py:120
  37.4 7.9 %copy-start = (bf16[4,256,128]{2,1,0:T(8,128)(2,1)}, bf16[4,256,128]{2,1,0:T(8,128)(2,1)S(1)}, u32[]{:S(2)}) copy-start(bf16[4,256,128]{2,1,0:T(8,128)(2,1)S(1)} %collective-permute-done.above_r) | copy-start | bytes 786436
  45.3 0.7 %copy-start.1 = (bf16[4,256,128]{2,1,0:T(8,128)(2,1)}, bf16[4,256,128]{2,1,0:T(8,128)(2,1)S(1)}, u32[]{:S(2)}) copy-start(bf16[4,256,128]{2,1,0:T(8,128)(2,1)S(1)} %collective-permute-done.1.below_r) | copy-start | bytes 786436

commit v2 on v1

--- a/solution.py
+++ b/solution.py
@@ -24,7 +24,10 @@
     return pl.pallas_call(
         body,
         out_shape=(half, half),
+        in_specs=[pl.BlockSpec(memory_space=pltpu.VMEM)],
+        out_specs=(pl.BlockSpec(memory_space=pltpu.VMEM),) * 2,
         scratch_shapes=[pltpu.VMEM((CH * ROWS, LANES), jnp.float32)],
+        compiler_params=pltpu.CompilerParams(vmem_limit_bytes=8 << 20),
         name="rows_first",
     )(stack)
 
@@ -100,11 +103,13 @@
     return pl.pallas_call(
         body,
         out_shape=jax.ShapeDtypeStruct((CH, ROWS, LANES), jnp.bfloat16),
+        in_specs=[pl.BlockSpec(memory_space=pltpu.VMEM)] * 8,
         scratch_shapes=[
             pltpu.VMEM((48, CH, LANES), jnp.bfloat16),
             pltpu.VMEM((16, 2 * CH, LANES), jnp.bfloat16),
             pltpu.VMEM((CH * ROWS, LANES), jnp.float32),
         ],
+        compiler_params=pltpu.CompilerParams(vmem_limit_bytes=16 << 20),
         name="merges",
     )(above, top, bottom, below, w_pair, w_mixed, slope_pair, slope_mixed)
 

time: 50.6 us -> 47.1 us (0.931)
  Pallas kernels: 6.32 us -> 3.25 us
    pallas_call x1, Pallas kernels: 2.05 us -> 0.23 us  [rows_first(): pl.pallas_call(body, out_shape=(half, half), in_specs=[pl.BlockSpec(memor...]
    pallas_call x1, Pallas kernels: 4.27 us -> 3.02 us  [merges(): pl.pallas_call(body, out_shape=jax.ShapeDtypeStruct((CH, ROWS, LANES), jn...]
where the time goes in v2:
time: 47.1 us; the launch traced here: 46.9 us
  blocking collectives  23.4 us (50%)
  starting transfers between devices  10.2 us (22%)
  waiting for transfers between devices  9.38 us (20%)
  Pallas kernels  3.25 us (7%)
  local copies, waits for them, and re-layouts  0.67 us (1%)
    all_to_all x1, blocking collectives, on_device(): lax.all_to_all(frames, 'frame', 0, 0, axis_index_groups=groups, tiled=True)  23.4 us
    ppermute x1, starting transfers between devices, on_device(): above = lax.ppermute(bottom, 'row', [(i, i + 1) for i in range(ends)])  8.3 us
    ppermute x1, waiting for transfers between devices, on_device(): below = lax.ppermute(top, 'row', [(i + 1, i) for i in range(ends)])  8.01 us
    pallas_call x1, Pallas kernels, merges(): pl.pallas_call(body, out_shape=jax.ShapeDtypeStruct((CH, ROWS, LANES), jn...  3.02 us
    ppermute x1, starting transfers between devices, on_device(): below = lax.ppermute(top, 'row', [(i + 1, i) for i in range(ends)])  1.92 us
    ppermute x1, waiting for transfers between devices, on_device(): above = lax.ppermute(bottom, 'row', [(i, i + 1) for i in range(ends)])  1.37 us
  transfers between devices with their start and end apart: 2, of which 2 were waited for; matrix products, arithmetic and copies ran while one was open for 0% of the time, Pallas kernels for 0%

profile of v2, /device:TPU:57, one launch (start us, length us, event | category | flops | bytes accessed | tf_op | source)
XLA Modules:
  0.0 46.9 jit_solution(14110857827185077142)
XLA Ops:
  0.0 23.4 %all_to_all.5.src = bf16[4,64,8,128]{3,2,1,0:T(8,128)(2,1)S(1)} all-to-all(bf16[4,64,8,128]{3,2,1,0:T(8,128)(2,1)} %param.5), channel_id=1, replica_groups={{0,4,8,12},{1,5,9,13},{2,6,10,14},{3,7,11,15},{16,20,24,28},{17,21,25,2..., dimensions={0} | all-to-all | bytes 1048576 | tf_op jit(solution)/shard_map/all_to_all | solution.py:121
  23.4 0.0 copy-start
  23.4 0.0 copy-start.1
  23.4 0.2 rows_first.1
  23.6 8.3 %collective-permute-start = (bf16[4,256,128]{2,1,0:T(8,128)(2,1)S(1)}, bf16[4,256,128]{2,1,0:T(8,128)(2,1)S(1)}, u32[]{:S(2)}, u32[]{:S(2)}) collective-permute-start(bf16[4,256,128]{2,1,0:T(8,128)(2,1)S(1)} %get-tuple-element.7.bottom_r), channel_id=1, source_target_pairs={{0,16},{16,32},{32,48},{48,64},{64,80},{80,96},{96,112},{112,128},... | collective-permute-start | bytes 786440 | tf_op jit(solution)/shard_map/ppermute | solution.py:124
  31.9 1.9 %collective-permute-start.1 = (bf16[4,256,128]{2,1,0:T(8,128)(2,1)S(1)}, bf16[4,256,128]{2,1,0:T(8,128)(2,1)S(1)}, u32[]{:S(2)}, u32[]{:S(2)}) collective-permute-start(bf16[4,256,128]{2,1,0:T(8,128)(2,1)S(1)} %get-tuple-element.8.top_r), channel_id=1, source_target_pairs={{16,0},{32,16},{48,32},{64,48},{80,64},{96,80},{112,96},{128,112},... | collective-permute-start | bytes 786440 | tf_op jit(solution)/shard_map/ppermute | solution.py:125
  33.8 1.4 %collective-permute-done.above_r = bf16[4,256,128]{2,1,0:T(8,128)(2,1)S(1)} collective-permute-done((bf16[4,256,128]{2,1,0:T(8,128)(2,1)S(1)}, bf16[4,256,128]{2,1,0:T(8,128)(2,1)S(1)}, u32[]{:S(2)}, u32[]{:S(2)}) %collective-permute-start) | collective-permute-done | bytes 262176 | tf_op jit(solution)/shard_map/ppermute | solution.py:124
  35.2 8.0 %collective-permute-done.1.below_r = bf16[4,256,128]{2,1,0:T(8,128)(2,1)S(1)} collective-permute-done((bf16[4,256,128]{2,1,0:T(8,128)(2,1)S(1)}, bf16[4,256,128]{2,1,0:T(8,128)(2,1)S(1)}, u32[]{:S(2)}, u32[]{:S(2)}) %collective-permute-start.1) | collective-permute-done | bytes 262176 | tf_op jit(solution)/shard_map/ppermute | solution.py:125
  43.2 0.0 copy-start.2
  43.2 0.0 copy-start.3
  43.2 0.0 copy-done
  43.2 0.0 copy-done.1
  43.2 0.6 %copy-done.2 = f32[64]{0:T(128)S(1)} copy-done((f32[64]{0:T(128)S(1)}, f32[64]{0:T(128)}, u32[]{:S(2)}) %copy-start.2) | copy-done | bytes 280
  43.9 0.0 copy-done.3
  43.9 3.0 %merges.1 = bf16[64,8,128]{2,1,0:T(8,128)(2,1)} custom-call(bf16[4,256,128]{2,1,0:T(8,128)(2,1)S(1)} %collective-permute-done.above_r, bf16[4,256,128]{2,1,0:T(8,128)(2,1)S(1)} %get-tuple-element.8.top_r, bf16[4,256,128]{2,1,0:T(8,128)(2,1)S(1)} %get-tuple-element.7.bottom_r, bf16[4,256,128]{2,1,0:T(8,128)(2,1)S(1)} %collective-permute-done.1.below_r, ...), custom_call_target="tpu_custom_call" | custom-call | tf_op jit(solution)/shard_map/merges/pallas_call | solution.py:103
Async XLA Ops:
  23.4 19.9 %copy-start = (bf16[3,3,64,128]{3,2,1,0:T(8,128)(2,1)S(1)}, bf16[3,3,64,128]{3,2,1,0:T(8,128)(2,1)}, u32[]{:S(2)}) copy-start(bf16[3,3,64,128]{3,2,1,0:T(8,128)(2,1)} %param.6) | copy-start | bytes 442372
  23.4 19.9 %copy-start.1 = (bf16[3,3,64,64]{3,2,1,0:T(8,128)(2,1)S(1)}, bf16[3,3,64,64]{3,2,1,0:T(8,128)(2,1)}, u32[]{:S(2)}) copy-start(bf16[3,3,64,64]{3,2,1,0:T(8,128)(2,1)} %param.7) | copy-start | bytes 221188
  23.6 11.6 %collective-permute-start = (bf16[4,256,128]{2,1,0:T(8,128)(2,1)S(1)}, bf16[4,256,128]{2,1,0:T(8,128)(2,1)S(1)}, u32[]{:S(2)}, u32[]{:S(2)}) collective-permute-start(bf16[4,256,128]{2,1,0:T(8,128)(2,1)S(1)} %get-tuple-element.7.bottom_r), channel_id=1, source_target_pairs={{0,16},{16,32},{32,48},{48,64},{64,80},{80,96},{96,112},{112,128},... | collective-permute-start | bytes 786440 | tf_op jit(solution)/shard_map/ppermute | solution.py:124
  31.9 11.3 %collective-permute-start.1 = (bf16[4,256,128]{2,1,0:T(8,128)(2,1)S(1)}, bf16[4,256,128]{2,1,0:T(8,128)(2,1)S(1)}, u32[]{:S(2)}, u32[]{:S(2)}) collective-permute-start(bf16[4,256,128]{2,1,0:T(8,128)(2,1)S(1)} %get-tuple-element.8.top_r), channel_id=1, source_target_pairs={{16,0},{32,16},{48,32},{64,48},{80,64},{96,80},{112,96},{128,112},... | collective-permute-start | bytes 786440 | tf_op jit(solution)/shard_map/ppermute | solution.py:125
  43.2 0.7 %copy-start.2 = (f32[64]{0:T(128)S(1)}, f32[64]{0:T(128)}, u32[]{:S(2)}) copy-start(f32[64]{0:T(128)} %param.8) | copy-start | bytes 772
  43.2 0.7 %copy-start.3 = (f32[64]{0:T(128)S(1)}, f32[64]{0:T(128)}, u32[]{:S(2)}) copy-start(f32[64]{0:T(128)} %param.9) | copy-start | bytes 772

commit v3 on v0

v3 whole, which is shorter than its diff:
```python
import jax
import jax.numpy as jnp
from jax import lax
from jax.experimental import pallas as pl
from jax.experimental.pallas import tpu as pltpu
from jax.sharding import PartitionSpec as P


ROWS = 8
HALO = 4
CH = 64
LANES = 128
VMEM = pl.BlockSpec(memory_space=pltpu.VMEM)
SMALL = pltpu.CompilerParams(vmem_limit_bytes=8 << 20)


def array(*shape, dtype=jnp.bfloat16):
    return jax.ShapeDtypeStruct(shape, dtype)


def spread(frames):
    def body(src, own, one, two, three, held, wide, sems):
        at = lax.axis_index("frame") // (lax.axis_size("frame") // 4)
        outs = (own, one, two, three)
        order = (1, 3, 2, 0)

        def copy(k):
            return pltpu.make_async_copy(src.at[(at + k) % 4], held.at[k], sems.at[k])

        for k in order:
            copy(k).start()
        for k in order:
            copy(k).wait()
            wide[k] = held[k].astype(jnp.float32).reshape(CH * ROWS, LANES)
            for row in range(ROWS):
                outs[k][row] = wide[k, pl.ds(row, CH, stride=ROWS), :].astype(jnp.bfloat16)

    return pl.pallas_call(
        body,
        out_shape=(array(ROWS, CH, LANES),) * 4,
        in_specs=[pl.BlockSpec(memory_space=pltpu.HBM)],
        out_specs=(VMEM,) * 4,
        scratch_shapes=[
            pltpu.VMEM((4, CH, ROWS, LANES), jnp.bfloat16),
            pltpu.VMEM((4, CH * ROWS, LANES), jnp.float32),
            pltpu.SemaphoreType.DMA((4,)),
        ],
        compiler_params=SMALL,
        name="spread",
    )(frames)


def weights(w_pair, w_mixed, slope_pair, slope_mixed):
    def body(wp, wm, sp, sm, pair, mixed, cols):
        for ky in range(3):
            at = ky * 2 * CH
            pair[0, :, at : at + 2 * CH] = wp[ky]
            pair[1, :, at : at + 2 * CH] = jnp.concatenate([wp[ky][:, CH:], wp[ky][:, :CH]], axis=1)
        mixed[...] = jnp.concatenate([wm[0], wm[1], wm[2]], axis=1)
        square = lax.broadcasted_iota(jnp.int32, (CH, CH), 0) == lax.broadcasted_iota(jnp.int32, (CH, CH), 1)
        for k, slope in enumerate((sp, sm)):
            column = jnp.sum(jnp.where(square, slope[...], 0.0), axis=1, keepdims=True)
            cols[k] = jnp.broadcast_to(column, (CH, LANES))

    return pl.pallas_call(
        body,
        out_shape=(array(2, 3 * CH, 6 * CH), array(3 * CH, 3 * CH), array(2, CH, LANES, dtype=jnp.float32)),
        in_specs=[VMEM] * 4,
        out_specs=(VMEM,) * 3,
        compiler_params=SMALL,
        name="weights",
    )(w_pair.reshape(3, 3 * CH, 2 * CH), w_mixed.reshape(3, 3 * CH, CH), slope_pair.reshape(1, CH), slope_mixed.reshape(1, CH))


def edges(*frames):
    def body(*refs):
        top, bottom = refs[-2:]
        for k, frame in enumerate(refs[:-2]):
            top[:, k * CH : (k + 1) * CH, :] = frame[:HALO]
            bottom[:, k * CH : (k + 1) * CH, :] = frame[HALO:]

    half = array(HALO, len(frames) * CH, LANES)
    return pl.pallas_call(
        body,
        out_shape=(half, half),
        in_specs=[VMEM] * len(frames),
        out_specs=(VMEM,) * 2,
        compiler_params=SMALL,
        name="edges",
    )(*frames)


class Level:
    def __init__(self, pair, mixed, cols, swap, hid):
        lane = lax.broadcasted_iota(jnp.int32, (CH, LANES), 1)
        self.not_first = lane > 0
        self.not_last = lane < LANES - 1
        self.pair = pair[swap]
        self.mixed = mixed[...]
        self.cols = cols
        self.swap = swap
        self.hid = hid
        self.place = lax.axis_index("row")
        self.last = lax.axis_size("row") - 1

    def inside(self, row, value):
        if row < HALO:
            return jnp.where(self.place > 0, value, 0.0)
        if row >= HALO + ROWS:
            return jnp.where(self.place < self.last, value, 0.0)
        return value

    def fold(self, part, which):
        left = jnp.where(self.not_first, pltpu.roll(part[:CH], 1, 1), 0.0)
        right = jnp.where(self.not_last, pltpu.roll(part[2 * CH :], LANES - 1, 1), 0.0)
        total = part[CH : 2 * CH] + left + right
        return jnp.where(total >= 0, total, self.cols[which] * total)

    def product(self, lhs, rows):
        rhs = jnp.concatenate([jnp.concatenate(rows[0:3], axis=0), jnp.concatenate(rows[1:4], axis=0)], axis=1)
        return jnp.dot(lhs, rhs, preferred_element_type=jnp.float32)

    def run(self, one, two, low, high, emit):
        for row in range(low - 1, high + 1, 2):
            rows = [jnp.concatenate([one(r), two(r)], axis=0) for r in range(row - 1, row + 3)]
            both = self.product(self.pair, rows)
            for k in range(2):
                value = self.fold(both[:, k * LANES : (k + 1) * LANES], 0)
                self.hid[row + k] = self.inside(row + k, value).astype(jnp.bfloat16)
        for row in range(low, high, 2):
            both = self.product(self.mixed, [self.hid[r] for r in range(row - 1, row + 3)])
            for k in range(2):
                first = jnp.where(self.swap > 0, two(row + k).astype(jnp.float32), one(row + k).astype(jnp.float32))
                branch = self.fold(both[:, k * LANES : (k + 1) * LANES], 1)
                emit(row + k, self.inside(row + k, first + branch))


def rows_of(above, frame, below, slot):
    def load(row):
        if row < HALO:
            return above[row, slot * CH : (slot + 1) * CH, :]
        if row < HALO + ROWS:
            return frame[row - HALO]
        return below[row - HALO - ROWS, slot * CH : (slot + 1) * CH, :]

    return load


def position():
    return lax.axis_index("frame") // (lax.axis_size("frame") // 4)


def merge_near(above, before, after, below, tables):
    def body(above_r, before_r, after_r, below_r, pair, mixed, cols, out, hid):
        at = position()
        swap = jnp.where((at == 0) | (at == 3), 1, 0)
        level = Level(pair, mixed, cols, swap, hid)

        def emit(row, value):
            out[row - 2] = value.astype(jnp.bfloat16)

        level.run(rows_of(above_r, before_r, below_r, 1), rows_of(above_r, after_r, below_r, 2), 2, 14, emit)

    return pl.pallas_call(
        body,
        out_shape=array(12, CH, LANES),
        in_specs=[VMEM] * 7,
        out_specs=VMEM,
        scratch_shapes=[pltpu.VMEM((16, CH, LANES), jnp.bfloat16)],
        compiler_params=SMALL,
        name="merge_near",
    )(above, before, after, below, *tables)


def merge_rest(above, own, below, above_far, far, below_far, near, tables):
    def body(above_r, own_r, below_r, above_far_r, far_r, below_far_r, near_r, pair, mixed, cols, out, hid, hid_two, mine, wide):
        at = position()
        level = Level(pair, mixed, cols, jnp.where(at >= 2, 1, 0), hid)

        def emit(row, value):
            mine[row - 2] = value.astype(jnp.bfloat16)

        level.run(rows_of(above_r, own_r, below_r, 0), rows_of(above_far_r, far_r, below_far_r, 0), 2, 14, emit)
        top = Level(pair, mixed, cols, at % 2, hid_two)

        def emit_two(row, value):
            wide[pl.ds(row - HALO, CH, stride=ROWS), :] = value

        top.run(lambda row: mine[row - 2], lambda row: near_r[row - 2], HALO, HALO + ROWS, emit_two)
        out[...] = wide[...].reshape(CH, ROWS, LANES).astype(jnp.bfloat16)

    return pl.pallas_call(
        body,
        out_shape=array(CH, ROWS, LANES),
        in_specs=[VMEM] * 10,
        scratch_shapes=[
            pltpu.VMEM((16, CH, LANES), jnp.bfloat16),
            pltpu.VMEM((16, CH, LANES), jnp.bfloat16),
            pltpu.VMEM((12, CH, LANES), jnp.bfloat16),
            pltpu.VMEM((CH * ROWS, LANES), jnp.float32),
        ],
        compiler_params=SMALL,
        name="merge_rest",
    )(above, own, below, above_far, far, below_far, near, *tables)


def on_device(frames, w_pair, w_mixed, slope_pair, slope_mixed):
    count = lax.axis_size("frame")
    quarter = count // 4
    ends = lax.axis_size("row") - 1

    def turned(block, by):
        return lax.ppermute(block, "frame", [(i, (i + by * quarter) % count) for i in range(count)])

    def halos(top, bottom):
        above = lax.ppermute(bottom, "row", [(i, i + 1) for i in range(ends)])
        below = lax.ppermute(top, "row", [(i + 1, i) for i in range(ends)])
        return above, below

    own, one, two, three = spread(frames)
    before = turned(one, 1)
    after = turned(three, 3)
    far = turned(two, 2)
    tables = weights(w_pair, w_mixed, slope_pair, slope_mixed)
    near_edges = edges(own, before, after)
    above, below = halos(*near_edges)
    far_edges = edges(far)
    above_far, below_far = halos(*far_edges)
    near = merge_near(above, before, after, below, tables)
    merged = merge_rest(above, own, below, above_far, far, below_far, near, tables)
    return merged[None]


def solution(mesh):
    placed = (P("frame", None, "row", None), P(), P(), P(), P())
    return jax.shard_map(
        on_device,
        mesh=mesh,
        in_specs=placed,
        out_specs=P("frame", None, "row", None),
        check_vma=False,
    )
```

time: 128 us -> 57.9 us (0.45)
  waiting for transfers between devices: 58.6 us -> 15.9 us
  matrix products: 13.5 us -> 0 us
  starting transfers between devices: 45.9 us -> 35.4 us
  other arithmetic: 7.09 us -> 0 us
  Pallas kernels: 0 us -> 4.4 us
    ppermute x10 -> x7, waiting for transfers between devices: 58.6 us -> 15.9 us  [the longest x3 10.4 us: turned(): lax.ppermute(block, 'frame', [(i, (i + by * quarter) % count) for i in ra...]
    dot_general x36 -> x0, matrix products: 13.5 us -> none  [convolve(): jnp.einsum('oc,fchw->fohw', weight[tap_y, tap_x], wide[:, :, tap_y:tap_y...]
    ppermute x10 -> x7, starting transfers between devices: 45.9 us -> 35.4 us  [the longest x3 18.8 us: turned(): lax.ppermute(block, 'frame', [(i, (i + by * quarter) % count) for i in ra...]
    concatenate x4 -> x0, other arithmetic: 5.73 us -> none  [padded_2(): jnp.concatenate([lax.ppermute(tail, axis, [(i, (i + 1) % count) for i in...]
    pallas_call x0 -> x6, Pallas kernels: none -> 4.4 us  [the longest x1 2.31 us: merge_rest(): pl.pallas_call(body, out_shape=array(CH, ROWS, LANES), in_specs=[VMEM] *...]
  transfers between devices with their start and end apart: 10 -> 7, of which waited for: 6 -> 4; matrix products, arithmetic and copies ran while one was open for 0% -> 0% of each run, Pallas kernels for 0% -> 2%
where the time goes in v3:
time: 57.9 us; the launch traced here: 57.6 us
  starting transfers between devices  35.4 us (61%)
  waiting for transfers between devices  15.9 us (27%)
  Pallas kernels  4.4 us (8%)
  local copies, waits for them, and re-layouts  1.69 us (3%)
    ppermute x3, starting transfers between devices, turned(): lax.ppermute(block, 'frame', [(i, (i + by * quarter) % count) for i in ra...  18.8 us
    ppermute x2, starting transfers between devices, halos(): above = lax.ppermute(bottom, 'row', [(i, i + 1) for i in range(ends)])  12.8 us
    ppermute x3, waiting for transfers between devices, turned(): lax.ppermute(block, 'frame', [(i, (i + by * quarter) % count) for i in ra...  10.4 us
    ppermute x2, waiting for transfers between devices, halos(): below = lax.ppermute(top, 'row', [(i + 1, i) for i in range(ends)])  5.42 us
    ppermute x2, starting transfers between devices, halos(): below = lax.ppermute(top, 'row', [(i + 1, i) for i in range(ends)])  3.84 us
    pallas_call x1, Pallas kernels, merge_rest(): pl.pallas_call(body, out_shape=array(CH, ROWS, LANES), in_specs=[VMEM] *...  2.31 us
    unnamed x10, local copies, waits for them, and re-layouts  1.69 us
  transfers between devices with their start and end apart: 7, of which 4 were waited for; matrix products, arithmetic and copies ran while one was open for 0% of the time, Pallas kernels for 2%

profile of v3, /device:TPU:57, one launch (start us, length us, event | category | flops | bytes accessed | tf_op | source)
XLA Modules:
  0.0 57.6 jit_solution(13442590673232877544)
XLA Ops:
  0.0 0.0 copy-start
  0.0 1.0 %copy-done = bf16[4,64,8,128]{3,2,1,0:T(8,128)(2,1)S(1)} copy-done((bf16[4,64,8,128]{3,2,1,0:T(8,128)(2,1)S(1)}, bf16[4,64,8,128]{3,2,1,0:T(8,128)(2,1)}, u32[]{:S(2)}) %copy-start) | copy-done | bytes 524312
  1.0 0.9 %spread.1 = (bf16[8,64,128]{2,1,0:T(8,128)(2,1)S(1)}, bf16[8,64,128]{2,1,0:T(8,128)(2,1)S(1)}, bf16[8,64,128]{2,1,0:T(8,128)(2,1)S(1)}, bf16[8,64,128]{2,1,0:T(8,128)(2,1)S(1)}) custom-call(bf16[4,64,8,128]{3,2,1,0:T(8,128)(2,1)S(1)} %copy-done), custom_call_target="tpu_custom_call" | custom-call | tf_op jit(solution)/shard_map/spread/pallas_call | solution.py:38
  2.0 5.8 %collective-permute-start = (bf16[8,64,128]{2,1,0:T(8,128)(2,1)S(1)}, bf16[8,64,128]{2,1,0:T(8,128)(2,1)S(1)}, u32[]{:S(2)}, u32[]{:S(2)}) collective-permute-start(bf16[8,64,128]{2,1,0:T(8,128)(2,1)S(1)} %get-tuple-element.17), channel_id=1, source_target_pairs={{0,4},{1,5},{2,6},{3,7},{4,8},{5,9},{6,10},{7,11},{8,12},{9,13},{1... | collective-permute-start | bytes 393224 | tf_op jit(solution)/shard_map/ppermute | solution.py:213
  7.8 6.8 %collective-permute-start.1 = (bf16[8,64,128]{2,1,0:T(8,128)(2,1)S(1)}, bf16[8,64,128]{2,1,0:T(8,128)(2,1)S(1)}, u32[]{:S(2)}, u32[]{:S(2)}) collective-permute-start(bf16[8,64,128]{2,1,0:T(8,128)(2,1)S(1)} %get-tuple-element.18), channel_id=1, source_target_pairs={{0,12},{1,13},{2,14},{3,15},{4,0},{5,1},{6,2},{7,3},{8,4},{9,5},{1... | collective-permute-start | bytes 393224 | tf_op jit(solution)/shard_map/ppermute | solution.py:213
  14.6 1.3 %collective-permute-done.refs_1_.before_r = bf16[8,64,128]{2,1,0:T(8,128)(2,1)S(1)} collective-permute-done((bf16[8,64,128]{2,1,0:T(8,128)(2,1)S(1)}, bf16[8,64,128]{2,1,0:T(8,128)(2,1)S(1)}, u32[]{:S(2)}, u32[]{:S(2)}) %collective-permute-start) | collective-permute-done | bytes 131104 | tf_op jit(solution)/shard_map/ppermute | solution.py:213
  15.9 4.4 %collective-permute-done.1.refs_2_.after_r = bf16[8,64,128]{2,1,0:T(8,128)(2,1)S(1)} collective-permute-done((bf16[8,64,128]{2,1,0:T(8,128)(2,1)S(1)}, bf16[8,64,128]{2,1,0:T(8,128)(2,1)S(1)}, u32[]{:S(2)}, u32[]{:S(2)}) %collective-permute-start.1) | collective-permute-done | bytes 131104 | tf_op jit(solution)/shard_map/ppermute | solution.py:213
  20.3 0.0 copy-start.2
  20.3 0.0 copy-start.1
  20.3 5.4 %collective-permute-start.2 = (bf16[4,192,128]{2,1,0:T(8,128)(2,1)S(1)}, bf16[4,192,128]{2,1,0:T(8,128)(2,1)S(1)}, u32[]{:S(2)}, u32[]{:S(2)}) collective-permute-start(bf16[4,192,128]{2,1,0:T(8,128)(2,1)S(1)} %get-tuple-element.19), channel_id=1, source_target_pairs={{0,16},{16,32},{32,48},{48,64},{64,80},{80,96},{96,112},{112,128},... | collective-permute-start | bytes 589832 | tf_op jit(solution)/shard_map/ppermute | solution.py:216
  25.7 1.9 %collective-permute-start.3 = (bf16[4,192,128]{2,1,0:T(8,128)(2,1)S(1)}, bf16[4,192,128]{2,1,0:T(8,128)(2,1)S(1)}, u32[]{:S(2)}, u32[]{:S(2)}) collective-permute-start(bf16[4,192,128]{2,1,0:T(8,128)(2,1)S(1)} %get-tuple-element.20), channel_id=1, source_target_pairs={{16,0},{32,16},{48,32},{64,48},{80,64},{96,80},{112,96},{128,112},... | collective-permute-start | bytes 589832 | tf_op jit(solution)/shard_map/ppermute | solution.py:217
  27.6 6.2 %collective-permute-start.4 = (bf16[8,64,128]{2,1,0:T(8,128)(2,1)S(1)}, bf16[8,64,128]{2,1,0:T(8,128)(2,1)S(1)}, u32[]{:S(2)}, u32[]{:S(2)}) collective-permute-start(bf16[8,64,128]{2,1,0:T(8,128)(2,1)S(1)} %get-tuple-element.21), channel_id=1, source_target_pairs={{0,8},{1,9},{2,10},{3,11},{4,12},{5,13},{6,14},{7,15},{8,0},{9,1},... | collective-permute-start | bytes 393224 | tf_op jit(solution)/shard_map/ppermute | solution.py:213
  33.9 4.7 %collective-permute-done.4.refs_0_.far_r = bf16[8,64,128]{2,1,0:T(8,128)(2,1)S(1)} collective-permute-done((bf16[8,64,128]{2,1,0:T(8,128)(2,1)S(1)}, bf16[8,64,128]{2,1,0:T(8,128)(2,1)S(1)}, u32[]{:S(2)}, u32[]{:S(2)}) %collective-permute-start.4) | collective-permute-done | bytes 131104 | tf_op jit(solution)/shard_map/ppermute | solution.py:213
  38.6 7.4 %collective-permute-start.5 = (bf16[4,64,128]{2,1,0:T(8,128)(2,1)S(1)}, bf16[4,64,128]{2,1,0:T(8,128)(2,1)S(1)}, u32[]{:S(2)}, u32[]{:S(2)}) collective-permute-start(bf16[4,64,128]{2,1,0:T(8,128)(2,1)S(1)} %get-tuple-element.22), channel_id=1, source_target_pairs={{0,16},{16,32},{32,48},{48,64},{64,80},{80,96},{96,112},{112,128},... | collective-permute-start | bytes 196616 | tf_op jit(solution)/shard_map/ppermute | solution.py:216
  46.1 1.9 %collective-permute-start.6 = (bf16[4,64,128]{2,1,0:T(8,128)(2,1)S(1)}, bf16[4,64,128]{2,1,0:T(8,128)(2,1)S(1)}, u32[]{:S(2)}, u32[]{:S(2)}) collective-permute-start(bf16[4,64,128]{2,1,0:T(8,128)(2,1)S(1)} %get-tuple-element.23), channel_id=1, source_target_pairs={{16,0},{32,16},{48,32},{64,48},{80,64},{96,80},{112,96},{128,112},... | collective-permute-start | bytes 196616 | tf_op jit(solution)/shard_map/ppermute | solution.py:217
  48.0 0.0 copy-start.3
  48.0 0.0 copy-start.4
  48.0 0.0 copy-done.2
  48.0 0.0 copy-done.1
  48.0 0.6 %copy-done.3 = f32[64]{0:T(128)S(1)} copy-done((f32[64]{0:T(128)S(1)}, f32[64]{0:T(128)}, u32[]{:S(2)}) %copy-start.3) | copy-done | bytes 280
  48.7 0.0 copy-done.4
  48.7 0.2 weights.1
  48.8 0.0 collective-permute-done.2.above_r
  48.8 0.0 collective-permute-done.3.below_r
  48.9 1.0 %merge_near.1.near_r = bf16[12,64,128]{2,1,0:T(8,128)(2,1)S(1)} custom-call(bf16[4,192,128]{2,1,0:T(8,128)(2,1)S(1)} %collective-permute-done.2.above_r, bf16[8,64,128]{2,1,0:T(8,128)(2,1)S(1)} %collective-permute-done.refs_1_.before_r, bf16[8,64,128]{2,1,0:T(8,128)(2,1)S(1)} %collective-permute-done.1.refs_2_.after_r, ...), custom_call_target="tpu_custom_call" | custom-call | tf_op jit(solution)/shard_map/merge_near/pallas_call | solution.py:164
  49.8 0.0 collective-permute-done.5.above_far_r
  49.8 5.4 %collective-permute-done.6.below_far_r = bf16[4,64,128]{2,1,0:T(8,128)(2,1)S(1)} collective-permute-done((bf16[4,64,128]{2,1,0:T(8,128)(2,1)S(1)}, bf16[4,64,128]{2,1,0:T(8,128)(2,1)S(1)}, u32[]{:S(2)}, u32[]{:S(2)}) %collective-permute-start.6) | collective-permute-done | bytes 65568 | tf_op jit(solution)/shard_map/ppermute | solution.py:217
  55.3 2.3 %merge_rest.1 = bf16[64,8,128]{2,1,0:T(8,128)(2,1)} custom-call(bf16[4,192,128]{2,1,0:T(8,128)(2,1)S(1)} %collective-permute-done.2.above_r, bf16[8,64,128]{2,1,0:T(8,128)(2,1)S(1)} %get-tuple-element.16.refs_0_.own_r, bf16[4,192,128]{2,1,0:T(8,128)(2,1)S(1)} %collective-permute-done.3.below_r, bf16[4,64,128]{2,1,0:T(8,128)(2,1)S(1)} %collective-permute-done.5.above_far_r, ...), custom_call_target="tpu_custom_call" | custom-call | tf_op jit(solution)/shard_map/merge_rest/pallas_call | solution.py:192
  (2 shorter events, 0.0 us)
Async XLA Ops:
  0.0 1.0 %copy-start = (bf16[4,64,8,128]{3,2,1,0:T(8,128)(2,1)S(1)}, bf16[4,64,8,128]{3,2,1,0:T(8,128)(2,1)}, u32[]{:S(2)}) copy-start(bf16[4,64,8,128]{3,2,1,0:T(8,128)(2,1)} %src.1) | copy-start | bytes 1572868
  2.0 13.9 %collective-permute-start = (bf16[8,64,128]{2,1,0:T(8,128)(2,1)S(1)}, bf16[8,64,128]{2,1,0:T(8,128)(2,1)S(1)}, u32[]{:S(2)}, u32[]{:S(2)}) collective-permute-start(bf16[8,64,128]{2,1,0:T(8,128)(2,1)S(1)} %get-tuple-element.17), channel_id=1, source_target_pairs={{0,4},{1,5},{2,6},{3,7},{4,8},{5,9},{6,10},{7,11},{8,12},{9,13},{1... | collective-permute-start | bytes 393224 | tf_op jit(solution)/shard_map/ppermute | solution.py:213
  7.8 12.5 %collective-permute-start.1 = (bf16[8,64,128]{2,1,0:T(8,128)(2,1)S(1)}, bf16[8,64,128]{2,1,0:T(8,128)(2,1)S(1)}, u32[]{:S(2)}, u32[]{:S(2)}) collective-permute-start(bf16[8,64,128]{2,1,0:T(8,128)(2,1)S(1)} %get-tuple-element.18), channel_id=1, source_target_pairs={{0,12},{1,13},{2,14},{3,15},{4,0},{5,1},{6,2},{7,3},{8,4},{9,5},{1... | collective-permute-start | bytes 393224 | tf_op jit(solution)/shard_map/ppermute | solution.py:213
  20.3 27.7 %copy-start.2 = (bf16[3,3,64,64]{3,2,1,0:T(8,128)(2,1)S(1)}, bf16[3,3,64,64]{3,2,1,0:T(8,128)(2,1)}, u32[]{:S(2)}) copy-start(bf16[3,3,64,64]{3,2,1,0:T(8,128)(2,1)} %param.7) | copy-start | bytes 221188
  20.3 27.7 %copy-start.1 = (bf16[3,3,64,128]{3,2,1,0:T(8,128)(2,1)S(1)}, bf16[3,3,64,128]{3,2,1,0:T(8,128)(2,1)}, u32[]{:S(2)}) copy-start(bf16[3,3,64,128]{3,2,1,0:T(8,128)(2,1)} %param.6) | copy-start | bytes 442372
  20.3 28.5 %collective-permute-start.2 = (bf16[4,192,128]{2,1,0:T(8,128)(2,1)S(1)}, bf16[4,192,128]{2,1,0:T(8,128)(2,1)S(1)}, u32[]{:S(2)}, u32[]{:S(2)}) collective-permute-start(bf16[4,192,128]{2,1,0:T(8,128)(2,1)S(1)} %get-tuple-element.19), channel_id=1, source_target_pairs={{0,16},{16,32},{32,48},{48,64},{64,80},{80,96},{96,112},{112,128},... | collective-permute-start | bytes 589832 | tf_op jit(solution)/shard_map/ppermute | solution.py:216
  25.7 23.1 %collective-permute-start.3 = (bf16[4,192,128]{2,1,0:T(8,128)(2,1)S(1)}, bf16[4,192,128]{2,1,0:T(8,128)(2,1)S(1)}, u32[]{:S(2)}, u32[]{:S(2)}) collective-permute-start(bf16[4,192,128]{2,1,0:T(8,128)(2,1)S(1)} %get-tuple-element.20), channel_id=1, source_target_pairs={{16,0},{32,16},{48,32},{64,48},{80,64},{96,80},{112,96},{128,112},... | collective-permute-start | bytes 589832 | tf_op jit(solution)/shard_map/ppermute | solution.py:217
  27.6 11.0 %collective-permute-start.4 = (bf16[8,64,128]{2,1,0:T(8,128)(2,1)S(1)}, bf16[8,64,128]{2,1,0:T(8,128)(2,1)S(1)}, u32[]{:S(2)}, u32[]{:S(2)}) collective-permute-start(bf16[8,64,128]{2,1,0:T(8,128)(2,1)S(1)} %get-tuple-element.21), channel_id=1, source_target_pairs={{0,8},{1,9},{2,10},{3,11},{4,12},{5,13},{6,14},{7,15},{8,0},{9,1},... | collective-permute-start | bytes 393224 | tf_op jit(solution)/shard_map/ppermute | solution.py:213
  38.6 11.2 %collective-permute-start.5 = (bf16[4,64,128]{2,1,0:T(8,128)(2,1)S(1)}, bf16[4,64,128]{2,1,0:T(8,128)(2,1)S(1)}, u32[]{:S(2)}, u32[]{:S(2)}) collective-permute-start(bf16[4,64,128]{2,1,0:T(8,128)(2,1)S(1)} %get-tuple-element.22), channel_id=1, source_target_pairs={{0,16},{16,32},{32,48},{48,64},{64,80},{80,96},{96,112},{112,128},... | collective-permute-start | bytes 196616 | tf_op jit(solution)/shard_map/ppermute | solution.py:216
  46.1 9.2 %collective-permute-start.6 = (bf16[4,64,128]{2,1,0:T(8,128)(2,1)S(1)}, bf16[4,64,128]{2,1,0:T(8,128)(2,1)S(1)}, u32[]{:S(2)}, u32[]{:S(2)}) collective-permute-start(bf16[4,64,128]{2,1,0:T(8,128)(2,1)S(1)} %get-tuple-element.23), channel_id=1, source_target_pairs={{16,0},{32,16},{48,32},{64,48},{80,64},{96,80},{112,96},{128,112},... | collective-permute-start | bytes 196616 | tf_op jit(solution)/shard_map/ppermute | solution.py:217
  48.0 0.7 %copy-start.3 = (f32[64]{0:T(128)S(1)}, f32[64]{0:T(128)}, u32[]{:S(2)}) copy-start(f32[64]{0:T(128)} %param.8) | copy-start | bytes 772
  48.0 0.7 %copy-start.4 = (f32[64]{0:T(128)S(1)}, f32[64]{0:T(128)}, u32[]{:S(2)}) copy-start(f32[64]{0:T(128)} %param.9) | copy-start | bytes 772

commit v4 on v3

v4 whole, which is shorter than its diff:
```python
import jax
import jax.numpy as jnp
from jax import lax
from jax.experimental import pallas as pl
from jax.experimental.pallas import tpu as pltpu
from jax.sharding import PartitionSpec as P


ROWS = 8
HALO = 4
CH = 64
LANES = 128
VMEM = pl.BlockSpec(memory_space=pltpu.VMEM)
SMALL = pltpu.CompilerParams(vmem_limit_bytes=8 << 20)


def array(*shape, dtype=jnp.bfloat16):
    return jax.ShapeDtypeStruct(shape, dtype)


def position():
    return lax.axis_index("frame") // (lax.axis_size("frame") // 4)


def spread(frames):
    def body(src, own, one, three, two, wide):
        at = position()
        for k, out in ((1, one), (3, three), (2, two), (0, own)):
            wide[k] = src[at ^ k].astype(jnp.float32).reshape(CH * ROWS, LANES)
            for row in range(ROWS):
                out[row] = wide[k, pl.ds(row, CH, stride=ROWS), :].astype(jnp.bfloat16)

    return pl.pallas_call(
        body,
        out_shape=(array(ROWS, CH, LANES),) * 4,
        in_specs=[VMEM],
        out_specs=(VMEM,) * 4,
        scratch_shapes=[pltpu.VMEM((4, CH * ROWS, LANES), jnp.float32)],
        compiler_params=SMALL,
        name="spread",
    )(frames)


def weights(w_pair, w_mixed, slope_pair, slope_mixed):
    def body(wp, wm, sp, sm, pair, mixed, cols):
        for ky in range(3):
            at = ky * 2 * CH
            pair[0, :, at : at + 2 * CH] = wp[ky]
            pair[1, :, at : at + 2 * CH] = jnp.concatenate([wp[ky][:, CH:], wp[ky][:, :CH]], axis=1)
        mixed[...] = jnp.concatenate([wm[0], wm[1], wm[2]], axis=1)
        square = lax.broadcasted_iota(jnp.int32, (CH, CH), 0) == lax.broadcasted_iota(jnp.int32, (CH, CH), 1)
        for k, slope in enumerate((sp, sm)):
            column = jnp.sum(jnp.where(square, slope[...], 0.0), axis=1, keepdims=True)
            cols[k] = jnp.broadcast_to(column, (CH, LANES))

    return pl.pallas_call(
        body,
        out_shape=(array(2, 3 * CH, 6 * CH), array(3 * CH, 3 * CH), array(2, CH, LANES, dtype=jnp.float32)),
        in_specs=[VMEM] * 4,
        out_specs=(VMEM,) * 3,
        compiler_params=SMALL,
        name="weights",
    )(w_pair.reshape(3, 3 * CH, 2 * CH), w_mixed.reshape(3, 3 * CH, CH), slope_pair.reshape(1, CH), slope_mixed.reshape(1, CH))


def edges(*frames):
    def body(*refs):
        near_side, far_side = refs[-2:]
        odd = lax.axis_index("row") % 2
        for k, frame in enumerate(refs[:-2]):
            near_side[:, k * CH : (k + 1) * CH, :] = frame[pl.ds(HALO - HALO * odd, HALO)]
            far_side[:, k * CH : (k + 1) * CH, :] = frame[pl.ds(HALO * odd, HALO)]

    half = array(HALO, len(frames) * CH, LANES)
    return pl.pallas_call(
        body,
        out_shape=(half, half),
        in_specs=[VMEM] * len(frames),
        out_specs=(VMEM,) * 2,
        compiler_params=SMALL,
        name="edges",
    )(*frames)


def fill(stack, slot, near_side, frame, far_side, part):
    odd = lax.axis_index("row") % 2
    to = slice(slot * CH, (slot + 1) * CH)
    of = slice(part * CH, (part + 1) * CH)
    stack[HALO : HALO + ROWS, to, :] = frame[...]
    stack[pl.ds((HALO + ROWS) * (1 - odd), HALO), to, :] = near_side[:, of, :]
    stack[pl.ds((HALO + ROWS) * odd, HALO), to, :] = far_side[:, of, :]


class Level:
    def __init__(self, pair, mixed, cols, swap, hid):
        lane = lax.broadcasted_iota(jnp.int32, (CH, LANES), 1)
        self.not_first = lane > 0
        self.not_last = lane < LANES - 1
        self.pair = pair[swap]
        self.mixed = mixed[...]
        self.cols = cols
        self.swap = swap
        self.hid = hid
        self.place = lax.axis_index("row")
        self.last = lax.axis_size("row") - 1

    def inside(self, row, value):
        if row < HALO:
            return jnp.where(self.place > 0, value, 0.0)
        if row >= HALO + ROWS:
            return jnp.where(self.place < self.last, value, 0.0)
        return value

    def fold(self, part, which):
        left = jnp.where(self.not_first, pltpu.roll(part[:CH], 1, 1), 0.0)
        right = jnp.where(self.not_last, pltpu.roll(part[2 * CH :], LANES - 1, 1), 0.0)
        total = part[CH : 2 * CH] + left + right
        return jnp.where(total >= 0, total, self.cols[which] * total)

    def product(self, lhs, stack, row, depth):
        rhs = jnp.concatenate([stack[r - 1 : r + 2].reshape(3 * depth, LANES) for r in (row, row + 1)], axis=1)
        return jnp.dot(lhs, rhs, preferred_element_type=jnp.float32)

    def run(self, stack, shift, low, high, emit):
        for row in range(low - 1, high + 1, 2):
            both = self.product(self.pair, stack, row - shift, 2 * CH)
            for k in range(2):
                value = self.fold(both[:, k * LANES : (k + 1) * LANES], 0)
                self.hid[row + k] = self.inside(row + k, value).astype(jnp.bfloat16)
        for row in range(low, high, 2):
            both = self.product(self.mixed, self.hid, row, CH)
            for k in range(2):
                first = stack[row + k - shift, pl.ds(self.swap * CH, CH), :].astype(jnp.float32)
                branch = self.fold(both[:, k * LANES : (k + 1) * LANES], 1)
                emit(row + k, self.inside(row + k, first + branch))


def merge_near(near_side, one, three, far_side, tables):
    def body(near_r, one_r, three_r, far_r, pair, mixed, cols, out, stack, hid):
        fill(stack, 0, near_r, one_r, far_r, 1)
        fill(stack, 1, near_r, three_r, far_r, 2)
        level = Level(pair, mixed, cols, position() // 2, hid)

        def emit(row, value):
            out[row - 2] = value.astype(jnp.bfloat16)

        level.run(stack, 0, 2, 14, emit)

    return pl.pallas_call(
        body,
        out_shape=array(12, CH, LANES),
        in_specs=[VMEM] * 7,
        out_specs=VMEM,
        scratch_shapes=[
            pltpu.VMEM((16, 2 * CH, LANES), jnp.bfloat16),
            pltpu.VMEM((16, CH, LANES), jnp.bfloat16),
        ],
        compiler_params=SMALL,
        name="merge_near",
    )(near_side, one, three, far_side, *tables)


def merge_rest(near_side, own, far_side, near_side_two, two, far_side_two, near, tables):
    def body(near_r, own_r, far_r, near_two_r, two_r, far_two_r, near_level, pair, mixed, cols, out, stack, ones, hid, hid_two, wide):
        fill(stack, 0, near_r, own_r, far_r, 0)
        fill(stack, 1, near_two_r, two_r, far_two_r, 0)
        ones[:, CH:, :] = near_level[...]
        level = Level(pair, mixed, cols, position() // 2, hid)

        def emit(row, value):
            ones[row - 2, :CH, :] = value.astype(jnp.bfloat16)

        level.run(stack, 0, 2, 14, emit)
        top = Level(pair, mixed, cols, position() % 2, hid_two)

        def emit_two(row, value):
            wide[pl.ds(row - HALO, CH, stride=ROWS), :] = value

        top.run(ones, 2, HALO, HALO + ROWS, emit_two)
        out[...] = wide[...].reshape(CH, ROWS, LANES).astype(jnp.bfloat16)

    return pl.pallas_call(
        body,
        out_shape=array(CH, ROWS, LANES),
        in_specs=[VMEM] * 10,
        scratch_shapes=[
            pltpu.VMEM((16, 2 * CH, LANES), jnp.bfloat16),
            pltpu.VMEM((12, 2 * CH, LANES), jnp.bfloat16),
            pltpu.VMEM((16, CH, LANES), jnp.bfloat16),
            pltpu.VMEM((16, CH, LANES), jnp.bfloat16),
            pltpu.VMEM((CH * ROWS, LANES), jnp.float32),
        ],
        compiler_params=SMALL,
        name="merge_rest",
    )(near_side, own, far_side, near_side_two, two, far_side_two, near, *tables)


def on_device(frames, w_pair, w_mixed, slope_pair, slope_mixed):
    count = lax.axis_size("frame")
    quarter = count // 4
    rows = lax.axis_size("row")

    def swapped(block, mask):
        return lax.ppermute(block, "frame", [(i, i ^ (mask * quarter)) for i in range(count)])

    def on_chip(block):
        return lax.ppermute(block, "row", [(i, i ^ 1) for i in range(rows)])

    def off_chip(block):
        return lax.ppermute(block, "row", [(i, ((i + 1) ^ 1) - 1) for i in range(1, rows - 1)])

    own, one, three, two = spread(frames)
    one = swapped(one, 1)
    three = swapped(three, 3)
    two = swapped(two, 2)
    tables = weights(w_pair, w_mixed, slope_pair, slope_mixed)
    near_side, far_side = edges(own, one, three)
    far_side = off_chip(far_side)
    near_side = on_chip(near_side)
    near_side_two, far_side_two = edges(two)
    far_side_two = off_chip(far_side_two)
    near_side_two = on_chip(near_side_two)
    near = merge_near(near_side, one, three, far_side, tables)
    merged = merge_rest(near_side, own, far_side, near_side_two, two, far_side_two, near, tables)
    return merged[None]


def solution(mesh):
    placed = (P("frame", None, "row", None), P(), P(), P(), P())
    return jax.shard_map(
        on_device,
        mesh=mesh,
        in_specs=placed,
        out_specs=P("frame", None, "row", None),
        check_vma=False,
    )
```

time: 57.9 us -> 54.6 us (0.943)
  the two profiles are of different devices: /device:TPU:57 before, /device:TPU:121 now
where the time goes in v4:
time: 54.6 us; the launch traced here: 54.3 us
  starting transfers between devices  30.9 us (57%)
  waiting for transfers between devices  17.8 us (33%)
  Pallas kernels  3.78 us (7%)
  local copies, waits for them, and re-layouts  1.69 us (3%)
    ppermute x3, starting transfers between devices, swapped(): lax.ppermute(block, 'frame', [(i, i ^ mask * quarter) for i in range(coun...  19.2 us
    ppermute x3, waiting for transfers between devices, swapped(): lax.ppermute(block, 'frame', [(i, i ^ mask * quarter) for i in range(coun...  13.5 us
    ppermute x2, starting transfers between devices, off_chip(): lax.ppermute(block, 'row', [(i, (i + 1 ^ 1) - 1) for i in range(1, rows -...  6.79 us
    ppermute x2, starting transfers between devices, on_chip(): return lax.ppermute(block, 'row', [(i, i ^ 1) for i in range(rows)])  4.9 us
    ppermute x2, waiting for transfers between devices, off_chip(): lax.ppermute(block, 'row', [(i, (i + 1 ^ 1) - 1) for i in range(1, rows -...  4.26 us
    pallas_call x1, Pallas kernels, merge_rest(): pl.pallas_call(body, out_shape=array(CH, ROWS, LANES), in_specs=[VMEM] *...  2.34 us
    unnamed x10, local copies, waits for them, and re-layouts  1.69 us
  transfers between devices with their start and end apart: 7, of which 3 were waited for; matrix products, arithmetic and copies ran while one was open for 0% of the time, Pallas kernels for 2%

profile of v4, /device:TPU:121, one launch (start us, length us, event | category | flops | bytes accessed | tf_op | source)
XLA Modules:
  0.0 54.3 jit_solution(711079642742432499)
XLA Ops:
  0.0 0.0 copy-start
  0.0 1.0 %copy-done = bf16[4,64,8,128]{3,2,1,0:T(8,128)(2,1)S(1)} copy-done((bf16[4,64,8,128]{3,2,1,0:T(8,128)(2,1)S(1)}, bf16[4,64,8,128]{3,2,1,0:T(8,128)(2,1)}, u32[]{:S(2)}) %copy-start) | copy-done | bytes 524312
  1.0 0.2 spread.1
  1.3 5.8 %collective-permute-start = (bf16[8,64,128]{2,1,0:T(8,128)(2,1)S(1)}, bf16[8,64,128]{2,1,0:T(8,128)(2,1)S(1)}, u32[]{:S(2)}, u32[]{:S(2)}) collective-permute-start(bf16[8,64,128]{2,1,0:T(8,128)(2,1)S(1)} %get-tuple-element.17), channel_id=1, source_target_pairs={{0,4},{1,5},{2,6},{3,7},{4,0},{5,1},{6,2},{7,3},{8,12},{9,13},{10,... | collective-permute-start | bytes 393224 | tf_op jit(solution)/shard_map/ppermute | solution.py:204
  7.1 6.1 %collective-permute-start.1 = (bf16[8,64,128]{2,1,0:T(8,128)(2,1)S(1)}, bf16[8,64,128]{2,1,0:T(8,128)(2,1)S(1)}, u32[]{:S(2)}, u32[]{:S(2)}) collective-permute-start(bf16[8,64,128]{2,1,0:T(8,128)(2,1)S(1)} %get-tuple-element.18), channel_id=1, source_target_pairs={{0,12},{1,13},{2,14},{3,15},{4,8},{5,9},{6,10},{7,11},{8,4},{9,5},... | collective-permute-start | bytes 393224 | tf_op jit(solution)/shard_map/ppermute | solution.py:204
  13.2 0.0 collective-permute-done.refs_1_.one_r
  13.2 6.7 %collective-permute-done.1.refs_2_.three_r = bf16[8,64,128]{2,1,0:T(8,128)(2,1)S(1)} collective-permute-done((bf16[8,64,128]{2,1,0:T(8,128)(2,1)S(1)}, bf16[8,64,128]{2,1,0:T(8,128)(2,1)S(1)}, u32[]{:S(2)}, u32[]{:S(2)}) %collective-permute-start.1) | collective-permute-done | bytes 131104 | tf_op jit(solution)/shard_map/ppermute | solution.py:204
  20.0 0.0 copy-start.2
  20.0 0.0 copy-start.1
  20.0 2.5 %collective-permute-start.2 = (bf16[4,192,128]{2,1,0:T(8,128)(2,1)S(1)}, bf16[4,192,128]{2,1,0:T(8,128)(2,1)S(1)}, u32[]{:S(2)}, u32[]{:S(2)}) collective-permute-start(bf16[4,192,128]{2,1,0:T(8,128)(2,1)S(1)} %get-tuple-element.19), channel_id=1, source_target_pairs={{0,16},{16,0},{32,48},{48,32},{64,80},{80,64},{96,112},{112,96},{1... | collective-permute-start | bytes 589832 | tf_op jit(solution)/shard_map/ppermute | solution.py:207
  22.6 3.8 %collective-permute-start.3 = (bf16[4,192,128]{2,1,0:T(8,128)(2,1)S(1)}, bf16[4,192,128]{2,1,0:T(8,128)(2,1)S(1)}, u32[]{:S(2)}, u32[]{:S(2)}) collective-permute-start(bf16[4,192,128]{2,1,0:T(8,128)(2,1)S(1)} %get-tuple-element.20), channel_id=1, source_target_pairs={{16,32},{32,16},{48,64},{64,48},{80,96},{96,80},{112,128},{128,112... | collective-permute-start | bytes 589832 | tf_op jit(solution)/shard_map/ppermute | solution.py:210
  26.3 7.3 %collective-permute-start.4 = (bf16[8,64,128]{2,1,0:T(8,128)(2,1)S(1)}, bf16[8,64,128]{2,1,0:T(8,128)(2,1)S(1)}, u32[]{:S(2)}, u32[]{:S(2)}) collective-permute-start(bf16[8,64,128]{2,1,0:T(8,128)(2,1)S(1)} %get-tuple-element.21), channel_id=1, source_target_pairs={{0,8},{1,9},{2,10},{3,11},{4,12},{5,13},{6,14},{7,15},{8,0},{9,1},... | collective-permute-start | bytes 393224 | tf_op jit(solution)/shard_map/ppermute | solution.py:204
  33.6 6.8 %collective-permute-done.4.refs_0_.two_r = bf16[8,64,128]{2,1,0:T(8,128)(2,1)S(1)} collective-permute-done((bf16[8,64,128]{2,1,0:T(8,128)(2,1)S(1)}, bf16[8,64,128]{2,1,0:T(8,128)(2,1)S(1)}, u32[]{:S(2)}, u32[]{:S(2)}) %collective-permute-start.4) | collective-permute-done | bytes 131104 | tf_op jit(solution)/shard_map/ppermute | solution.py:204
  40.4 2.4 %collective-permute-start.5 = (bf16[4,64,128]{2,1,0:T(8,128)(2,1)S(1)}, bf16[4,64,128]{2,1,0:T(8,128)(2,1)S(1)}, u32[]{:S(2)}, u32[]{:S(2)}) collective-permute-start(bf16[4,64,128]{2,1,0:T(8,128)(2,1)S(1)} %get-tuple-element.22), channel_id=1, source_target_pairs={{0,16},{16,0},{32,48},{48,32},{64,80},{80,64},{96,112},{112,96},{1... | collective-permute-start | bytes 196616 | tf_op jit(solution)/shard_map/ppermute | solution.py:207
  42.8 3.0 %collective-permute-start.6 = (bf16[4,64,128]{2,1,0:T(8,128)(2,1)S(1)}, bf16[4,64,128]{2,1,0:T(8,128)(2,1)S(1)}, u32[]{:S(2)}, u32[]{:S(2)}) collective-permute-start(bf16[4,64,128]{2,1,0:T(8,128)(2,1)S(1)} %get-tuple-element.23), channel_id=1, source_target_pairs={{16,32},{32,16},{48,64},{64,48},{80,96},{96,80},{112,128},{128,112... | collective-permute-start | bytes 196616 | tf_op jit(solution)/shard_map/ppermute | solution.py:210
  45.8 0.0 copy-start.3
  45.8 0.0 copy-start.4
  45.9 0.0 copy-done.2
  45.9 0.0 copy-done.1
  45.9 0.6 %copy-done.3 = f32[64]{0:T(128)S(1)} copy-done((f32[64]{0:T(128)S(1)}, f32[64]{0:T(128)}, u32[]{:S(2)}) %copy-start.3) | copy-done | bytes 280
  46.5 0.0 copy-done.4
  46.5 0.2 weights.1
  46.7 0.0 collective-permute-done.2.near_r
  46.7 0.0 collective-permute-done.3.far_r
  46.7 1.0 %merge_near.1.near_level = bf16[12,64,128]{2,1,0:T(8,128)(2,1)S(1)} custom-call(bf16[4,192,128]{2,1,0:T(8,128)(2,1)S(1)} %collective-permute-done.2.near_r, bf16[8,64,128]{2,1,0:T(8,128)(2,1)S(1)} %collective-permute-done.refs_1_.one_r, bf16[8,64,128]{2,1,0:T(8,128)(2,1)S(1)} %collective-permute-done.1.refs_2_.three_r, ...), custom_call_target="tpu_custom_call" | custom-call | tf_op jit(solution)/shard_map/merge_near/pallas_call | solution.py:149
  47.7 0.0 collective-permute-done.5.near_two_r
  47.7 4.3 %collective-permute-done.6.far_two_r = bf16[4,64,128]{2,1,0:T(8,128)(2,1)S(1)} collective-permute-done((bf16[4,64,128]{2,1,0:T(8,128)(2,1)S(1)}, bf16[4,64,128]{2,1,0:T(8,128)(2,1)S(1)}, u32[]{:S(2)}, u32[]{:S(2)}) %collective-permute-start.6) | collective-permute-done | bytes 65568 | tf_op jit(solution)/shard_map/ppermute | solution.py:210
  52.0 2.3 %merge_rest.1 = bf16[64,8,128]{2,1,0:T(8,128)(2,1)} custom-call(bf16[4,192,128]{2,1,0:T(8,128)(2,1)S(1)} %collective-permute-done.2.near_r, bf16[8,64,128]{2,1,0:T(8,128)(2,1)S(1)} %get-tuple-element.16.refs_0_.own_r, bf16[4,192,128]{2,1,0:T(8,128)(2,1)S(1)} %collective-permute-done.3.far_r, bf16[4,64,128]{2,1,0:T(8,128)(2,1)S(1)} %collective-permute-done.5.near_two_r, ...), custom_call_target="tpu_custom_call" | custom-call | tf_op jit(solution)/shard_map/merge_rest/pallas_call | solution.py:182
  (2 shorter events, 0.0 us)
Async XLA Ops:
  0.0 1.0 %copy-start = (bf16[4,64,8,128]{3,2,1,0:T(8,128)(2,1)S(1)}, bf16[4,64,8,128]{3,2,1,0:T(8,128)(2,1)}, u32[]{:S(2)}) copy-start(bf16[4,64,8,128]{3,2,1,0:T(8,128)(2,1)} %src.1) | copy-start | bytes 1572868
  1.3 11.9 %collective-permute-start = (bf16[8,64,128]{2,1,0:T(8,128)(2,1)S(1)}, bf16[8,64,128]{2,1,0:T(8,128)(2,1)S(1)}, u32[]{:S(2)}, u32[]{:S(2)}) collective-permute-start(bf16[8,64,128]{2,1,0:T(8,128)(2,1)S(1)} %get-tuple-element.17), channel_id=1, source_target_pairs={{0,4},{1,5},{2,6},{3,7},{4,0},{5,1},{6,2},{7,3},{8,12},{9,13},{10,... | collective-permute-start | bytes 393224 | tf_op jit(solution)/shard_map/ppermute | solution.py:204
  7.1 12.9 %collective-permute-start.1 = (bf16[8,64,128]{2,1,0:T(8,128)(2,1)S(1)}, bf16[8,64,128]{2,1,0:T(8,128)(2,1)S(1)}, u32[]{:S(2)}, u32[]{:S(2)}) collective-permute-start(bf16[8,64,128]{2,1,0:T(8,128)(2,1)S(1)} %get-tuple-element.18), channel_id=1, source_target_pairs={{0,12},{1,13},{2,14},{3,15},{4,8},{5,9},{6,10},{7,11},{8,4},{9,5},... | collective-permute-start | bytes 393224 | tf_op jit(solution)/shard_map/ppermute | solution.py:204
  20.0 25.9 %copy-start.2 = (bf16[3,3,64,64]{3,2,1,0:T(8,128)(2,1)S(1)}, bf16[3,3,64,64]{3,2,1,0:T(8,128)(2,1)}, u32[]{:S(2)}) copy-start(bf16[3,3,64,64]{3,2,1,0:T(8,128)(2,1)} %param.7) | copy-start | bytes 221188
  20.0 25.9 %copy-start.1 = (bf16[3,3,64,128]{3,2,1,0:T(8,128)(2,1)S(1)}, bf16[3,3,64,128]{3,2,1,0:T(8,128)(2,1)}, u32[]{:S(2)}) copy-start(bf16[3,3,64,128]{3,2,1,0:T(8,128)(2,1)} %param.6) | copy-start | bytes 442372
  20.0 26.7 %collective-permute-start.2 = (bf16[4,192,128]{2,1,0:T(8,128)(2,1)S(1)}, bf16[4,192,128]{2,1,0:T(8,128)(2,1)S(1)}, u32[]{:S(2)}, u32[]{:S(2)}) collective-permute-start(bf16[4,192,128]{2,1,0:T(8,128)(2,1)S(1)} %get-tuple-element.19), channel_id=1, source_target_pairs={{0,16},{16,0},{32,48},{48,32},{64,80},{80,64},{96,112},{112,96},{1... | collective-permute-start | bytes 589832 | tf_op jit(solution)/shard_map/ppermute | solution.py:207
  22.6 24.1 %collective-permute-start.3 = (bf16[4,192,128]{2,1,0:T(8,128)(2,1)S(1)}, bf16[4,192,128]{2,1,0:T(8,128)(2,1)S(1)}, u32[]{:S(2)}, u32[]{:S(2)}) collective-permute-start(bf16[4,192,128]{2,1,0:T(8,128)(2,1)S(1)} %get-tuple-element.20), channel_id=1, source_target_pairs={{16,32},{32,16},{48,64},{64,48},{80,96},{96,80},{112,128},{128,112... | collective-permute-start | bytes 589832 | tf_op jit(solution)/shard_map/ppermute | solution.py:210
  26.3 14.1 %collective-permute-start.4 = (bf16[8,64,128]{2,1,0:T(8,128)(2,1)S(1)}, bf16[8,64,128]{2,1,0:T(8,128)(2,1)S(1)}, u32[]{:S(2)}, u32[]{:S(2)}) collective-permute-start(bf16[8,64,128]{2,1,0:T(8,128)(2,1)S(1)} %get-tuple-element.21), channel_id=1, source_target_pairs={{0,8},{1,9},{2,10},{3,11},{4,12},{5,13},{6,14},{7,15},{8,0},{9,1},... | collective-permute-start | bytes 393224 | tf_op jit(solution)/shard_map/ppermute | solution.py:204
  40.4 7.3 %collective-permute-start.5 = (bf16[4,64,128]{2,1,0:T(8,128)(2,1)S(1)}, bf16[4,64,128]{2,1,0:T(8,128)(2,1)S(1)}, u32[]{:S(2)}, u32[]{:S(2)}) collective-permute-start(bf16[4,64,128]{2,1,0:T(8,128)(2,1)S(1)} %get-tuple-element.22), channel_id=1, source_target_pairs={{0,16},{16,0},{32,48},{48,32},{64,80},{80,64},{96,112},{112,96},{1... | collective-permute-start | bytes 196616 | tf_op jit(solution)/shard_map/ppermute | solution.py:207
  42.8 9.2 %collective-permute-start.6 = (bf16[4,64,128]{2,1,0:T(8,128)(2,1)S(1)}, bf16[4,64,128]{2,1,0:T(8,128)(2,1)S(1)}, u32[]{:S(2)}, u32[]{:S(2)}) collective-permute-start(bf16[4,64,128]{2,1,0:T(8,128)(2,1)S(1)} %get-tuple-element.23), channel_id=1, source_target_pairs={{16,32},{32,16},{48,64},{64,48},{80,96},{96,80},{112,128},{128,112... | collective-permute-start | bytes 196616 | tf_op jit(solution)/shard_map/ppermute | solution.py:210
  45.8 0.7 %copy-start.3 = (f32[64]{0:T(128)S(1)}, f32[64]{0:T(128)}, u32[]{:S(2)}) copy-start(f32[64]{0:T(128)} %param.8) | copy-start | bytes 772
  45.8 0.7 %copy-start.4 = (f32[64]{0:T(128)S(1)}, f32[64]{0:T(128)}, u32[]{:S(2)}) copy-start(f32[64]{0:T(128)} %param.9) | copy-start | bytes 772

commit v5 on v4

--- a/solution.py
+++ b/solution.py
@@ -135,64 +135,40 @@
                 emit(row + k, self.inside(row + k, first + branch))
 
 
-def merge_near(near_side, one, three, far_side, tables):
-    def body(near_r, one_r, three_r, far_r, pair, mixed, cols, out, stack, hid):
-        fill(stack, 0, near_r, one_r, far_r, 1)
-        fill(stack, 1, near_r, three_r, far_r, 2)
-        level = Level(pair, mixed, cols, position() // 2, hid)
-
-        def emit(row, value):
-            out[row - 2] = value.astype(jnp.bfloat16)
-
-        level.run(stack, 0, 2, 14, emit)
-
-    return pl.pallas_call(
-        body,
-        out_shape=array(12, CH, LANES),
-        in_specs=[VMEM] * 7,
-        out_specs=VMEM,
+def merges(sides_early, sides_late, own, one, two, three, tables):
+    def body(near_a, far_a, near_b, far_b, own_r, one_r, two_r, three_r, pair, mixed, cols, out, stack, other, ones, hid, wide):
+        fill(other, 0, near_a, one_r, far_a, 1)
+        fill(other, 1, near_b, three_r, far_b, 1)
+        fill(stack, 0, near_a, own_r, far_a, 0)
+        fill(stack, 1, near_b, two_r, far_b, 0)
+        at = position()
+        for k, rows in ((1, other), (0, stack)):
+
+            def emit(row, value, k=k):
+                ones[row - 2, k * CH : (k + 1) * CH, :] = value.astype(jnp.bfloat16)
+
+            Level(pair, mixed, cols, at // 2, hid.at[k]).run(rows, 0, 2, 14, emit)
+
+        def emit_two(row, value):
+            wide[pl.ds(row - HALO, CH, stride=ROWS), :] = value
+
+        Level(pair, mixed, cols, at % 2, hid.at[2]).run(ones, 2, HALO, HALO + ROWS, emit_two)
+        out[...] = wide[...].reshape(CH, ROWS, LANES).astype(jnp.bfloat16)
+
+    return pl.pallas_call(
+        body,
+        out_shape=array(CH, ROWS, LANES),
+        in_specs=[VMEM] * 11,
         scratch_shapes=[
             pltpu.VMEM((16, 2 * CH, LANES), jnp.bfloat16),
-            pltpu.VMEM((16, CH, LANES), jnp.bfloat16),
-        ],
-        compiler_params=SMALL,
-        name="merge_near",
-    )(near_side, one, three, far_side, *tables)
-
-
-def merge_rest(near_side, own, far_side, near_side_two, two, far_side_two, near, tables):
-    def body(near_r, own_r, far_r, near_two_r, two_r, far_two_r, near_level, pair, mixed, cols, out, stack, ones, hid, hid_two, wide):
-        fill(stack, 0, near_r, own_r, far_r, 0)
-        fill(stack, 1, near_two_r, two_r, far_two_r, 0)
-        ones[:, CH:, :] = near_level[...]
-        level = Level(pair, mixed, cols, position() // 2, hid)
-
-        def emit(row, value):
-            ones[row - 2, :CH, :] = value.astype(jnp.bfloat16)
-
-        level.run(stack, 0, 2, 14, emit)
-        top = Level(pair, mixed, cols, position() % 2, hid_two)
-
-        def emit_two(row, value):
-            wide[pl.ds(row - HALO, CH, stride=ROWS), :] = value
-
-        top.run(ones, 2, HALO, HALO + ROWS, emit_two)
-        out[...] = wide[...].reshape(CH, ROWS, LANES).astype(jnp.bfloat16)
-
-    return pl.pallas_call(
-        body,
-        out_shape=array(CH, ROWS, LANES),
-        in_specs=[VMEM] * 10,
-        scratch_shapes=[
             pltpu.VMEM((16, 2 * CH, LANES), jnp.bfloat16),
             pltpu.VMEM((12, 2 * CH, LANES), jnp.bfloat16),
-            pltpu.VMEM((16, CH, LANES), jnp.bfloat16),
-            pltpu.VMEM((16, CH, LANES), jnp.bfloat16),
+            pltpu.VMEM((3, 16, CH, LANES), jnp.bfloat16),
             pltpu.VMEM((CH * ROWS, LANES), jnp.float32),
         ],
         compiler_params=SMALL,
-        name="merge_rest",
-    )(near_side, own, far_side, near_side_two, two, far_side_two, near, *tables)
+        name="merges",
+    )(*sides_early, *sides_late, own, one, two, three, *tables)
 
 
 def on_device(frames, w_pair, w_mixed, slope_pair, slope_mixed):
@@ -214,14 +190,13 @@
     three = swapped(three, 3)
     two = swapped(two, 2)
     tables = weights(w_pair, w_mixed, slope_pair, slope_mixed)
-    near_side, far_side = edges(own, one, three)
-    far_side = off_chip(far_side)
-    near_side = on_chip(near_side)
-    near_side_two, far_side_two = edges(two)
-    far_side_two = off_chip(far_side_two)
-    near_side_two = on_chip(near_side_two)
-    near = merge_near(near_side, one, three, far_side, tables)
-    merged = merge_rest(near_side, own, far_side, near_side_two, two, far_side_two, near, tables)
+    near_early, far_early = edges(own, one)
+    far_early = off_chip(far_early)
+    near_early = on_chip(near_early)
+    near_late, far_late = edges(two, three)
+    far_late = off_chip(far_late)
+    near_late = on_chip(near_late)
+    merged = merges((near_early, far_early), (near_late, far_late), own, one, two, three, tables)
     return merged[None]
 
 

time: 54.6 us -> 48 us (0.88)
  the two profiles are of different devices: /device:TPU:121 before, /device:TPU:6 now
where the time goes in v5:
time: 48 us; the launch traced here: 47.7 us
  starting transfers between devices  30.8 us (64%)
  waiting for transfers between devices  11.5 us (24%)
  Pallas kernels  3.53 us (7%)
  local copies, waits for them, and re-layouts  1.69 us (4%)
    ppermute x3, starting transfers between devices, swapped(): lax.ppermute(block, 'frame', [(i, i ^ mask * quarter) for i in range(coun...  17.1 us
    ppermute x2, starting transfers between devices, off_chip(): lax.ppermute(block, 'row', [(i, (i + 1 ^ 1) - 1) for i in range(1, rows -...  9.68 us
    ppermute x3, waiting for transfers between devices, swapped(): lax.ppermute(block, 'frame', [(i, i ^ mask * quarter) for i in range(coun...  5.84 us
    ppermute x2, waiting for transfers between devices, off_chip(): lax.ppermute(block, 'row', [(i, (i + 1 ^ 1) - 1) for i in range(1, rows -...  5.67 us
    ppermute x2, starting transfers between devices, on_chip(): return lax.ppermute(block, 'row', [(i, i ^ 1) for i in range(rows)])  3.97 us
    pallas_call x1, Pallas kernels, merges(): pl.pallas_call(body, out_shape=array(CH, ROWS, LANES), in_specs=[VMEM] *...  3.09 us
    unnamed x10, local copies, waits for them, and re-layouts  1.69 us
  transfers between devices with their start and end apart: 7, of which 2 were waited for; matrix products, arithmetic and copies ran while one was open for 0% of the time, Pallas kernels for 0%

profile of v5, /device:TPU:6, one launch (start us, length us, event | category | flops | bytes accessed | tf_op | source)
XLA Modules:
  0.0 47.7 jit_solution(10508189040782180917)
XLA Ops:
  0.0 0.0 copy-start
  0.0 1.0 %copy-done = bf16[4,64,8,128]{3,2,1,0:T(8,128)(2,1)S(1)} copy-done((bf16[4,64,8,128]{3,2,1,0:T(8,128)(2,1)S(1)}, bf16[4,64,8,128]{3,2,1,0:T(8,128)(2,1)}, u32[]{:S(2)}) %copy-start) | copy-done | bytes 524312
  1.0 0.2 spread.1
  1.3 10.9 %collective-permute-start.3 = (bf16[8,64,128]{2,1,0:T(8,128)(2,1)S(1)}, bf16[8,64,128]{2,1,0:T(8,128)(2,1)S(1)}, u32[]{:S(2)}, u32[]{:S(2)}) collective-permute-start(bf16[8,64,128]{2,1,0:T(8,128)(2,1)S(1)} %get-tuple-element.20), channel_id=1, source_target_pairs={{0,8},{1,9},{2,10},{3,11},{4,12},{5,13},{6,14},{7,15},{8,0},{9,1},... | collective-permute-start | bytes 393224 | tf_op jit(solution)/shard_map/ppermute | solution.py:180
  12.2 1.9 %collective-permute-start.4 = (bf16[8,64,128]{2,1,0:T(8,128)(2,1)S(1)}, bf16[8,64,128]{2,1,0:T(8,128)(2,1)S(1)}, u32[]{:S(2)}, u32[]{:S(2)}) collective-permute-start(bf16[8,64,128]{2,1,0:T(8,128)(2,1)S(1)} %get-tuple-element.21), channel_id=1, source_target_pairs={{0,12},{1,13},{2,14},{3,15},{4,8},{5,9},{6,10},{7,11},{8,4},{9,5},... | collective-permute-start | bytes 393224 | tf_op jit(solution)/shard_map/ppermute | solution.py:180
  14.2 4.3 %collective-permute-start = (bf16[8,64,128]{2,1,0:T(8,128)(2,1)S(1)}, bf16[8,64,128]{2,1,0:T(8,128)(2,1)S(1)}, u32[]{:S(2)}, u32[]{:S(2)}) collective-permute-start(bf16[8,64,128]{2,1,0:T(8,128)(2,1)S(1)} %get-tuple-element.17), channel_id=1, source_target_pairs={{0,4},{1,5},{2,6},{3,7},{4,0},{5,1},{6,2},{7,3},{8,12},{9,13},{10,... | collective-permute-start | bytes 393224 | tf_op jit(solution)/shard_map/ppermute | solution.py:180
  18.4 0.0 collective-permute-done.3.refs_0_.two_r
  18.4 5.8 %collective-permute-done.4.refs_1_.three_r = bf16[8,64,128]{2,1,0:T(8,128)(2,1)S(1)} collective-permute-done((bf16[8,64,128]{2,1,0:T(8,128)(2,1)S(1)}, bf16[8,64,128]{2,1,0:T(8,128)(2,1)S(1)}, u32[]{:S(2)}, u32[]{:S(2)}) %collective-permute-start.4) | collective-permute-done | bytes 131104 | tf_op jit(solution)/shard_map/ppermute | solution.py:180
  24.3 0.0 copy-start.2
  24.3 0.0 copy-start.1
  24.3 2.1 %collective-permute-start.5 = (bf16[4,128,128]{2,1,0:T(8,128)(2,1)S(1)}, bf16[4,128,128]{2,1,0:T(8,128)(2,1)S(1)}, u32[]{:S(2)}, u32[]{:S(2)}) collective-permute-start(bf16[4,128,128]{2,1,0:T(8,128)(2,1)S(1)} %get-tuple-element.22), channel_id=1, source_target_pairs={{0,16},{16,0},{32,48},{48,32},{64,80},{80,64},{96,112},{112,96},{1... | collective-permute-start | bytes 393224 | tf_op jit(solution)/shard_map/ppermute | solution.py:183
  26.4 6.3 %collective-permute-start.6 = (bf16[4,128,128]{2,1,0:T(8,128)(2,1)S(1)}, bf16[4,128,128]{2,1,0:T(8,128)(2,1)S(1)}, u32[]{:S(2)}, u32[]{:S(2)}) collective-permute-start(bf16[4,128,128]{2,1,0:T(8,128)(2,1)S(1)} %get-tuple-element.23), channel_id=1, source_target_pairs={{16,32},{32,16},{48,64},{64,48},{80,96},{96,80},{112,128},{128,112... | collective-permute-start | bytes 393224 | tf_op jit(solution)/shard_map/ppermute | solution.py:186
  32.7 0.0 collective-permute-done.refs_1_.one_r
  32.8 1.9 %collective-permute-start.1 = (bf16[4,128,128]{2,1,0:T(8,128)(2,1)S(1)}, bf16[4,128,128]{2,1,0:T(8,128)(2,1)S(1)}, u32[]{:S(2)}, u32[]{:S(2)}) collective-permute-start(bf16[4,128,128]{2,1,0:T(8,128)(2,1)S(1)} %get-tuple-element.18), channel_id=1, source_target_pairs={{0,16},{16,0},{32,48},{48,32},{64,80},{80,64},{96,112},{112,96},{1... | collective-permute-start | bytes 393224 | tf_op jit(solution)/shard_map/ppermute | solution.py:183
  34.7 3.4 %collective-permute-start.2 = (bf16[4,128,128]{2,1,0:T(8,128)(2,1)S(1)}, bf16[4,128,128]{2,1,0:T(8,128)(2,1)S(1)}, u32[]{:S(2)}, u32[]{:S(2)}) collective-permute-start(bf16[4,128,128]{2,1,0:T(8,128)(2,1)S(1)} %get-tuple-element.19), channel_id=1, source_target_pairs={{16,32},{32,16},{48,64},{64,48},{80,96},{96,80},{112,128},{128,112... | collective-permute-start | bytes 393224 | tf_op jit(solution)/shard_map/ppermute | solution.py:186
  38.0 0.0 copy-start.3
  38.1 0.0 copy-start.4
  38.1 0.0 copy-done.2
  38.1 0.0 copy-done.1
  38.1 0.6 %copy-done.3 = f32[64]{0:T(128)S(1)} copy-done((f32[64]{0:T(128)S(1)}, f32[64]{0:T(128)}, u32[]{:S(2)}) %copy-start.3) | copy-done | bytes 280
  38.7 0.0 copy-done.4
  38.7 0.2 weights.1
  38.9 0.0 collective-permute-done.5.near_b
  38.9 0.0 collective-permute-done.6.far_b
  38.9 0.0 collective-permute-done.1.near_a
  38.9 5.7 %collective-permute-done.2.far_a = bf16[4,128,128]{2,1,0:T(8,128)(2,1)S(1)} collective-permute-done((bf16[4,128,128]{2,1,0:T(8,128)(2,1)S(1)}, bf16[4,128,128]{2,1,0:T(8,128)(2,1)S(1)}, u32[]{:S(2)}, u32[]{:S(2)}) %collective-permute-start.2) | collective-permute-done | bytes 131104 | tf_op jit(solution)/shard_map/ppermute | solution.py:186
  44.6 3.1 %merges.1 = bf16[64,8,128]{2,1,0:T(8,128)(2,1)} custom-call(bf16[4,128,128]{2,1,0:T(8,128)(2,1)S(1)} %collective-permute-done.1.near_a, bf16[4,128,128]{2,1,0:T(8,128)(2,1)S(1)} %collective-permute-done.2.far_a, bf16[4,128,128]{2,1,0:T(8,128)(2,1)S(1)} %collective-permute-done.5.near_b, bf16[4,128,128]{2,1,0:T(8,128)(2,1)S(1)} %collective-permute-done.6.far_b, ...), custom_call_target="tpu_custom_call" | custom-call | tf_op jit(solution)/shard_map/merges/pallas_call | solution.py:158
  (2 shorter events, 0.1 us)
Async XLA Ops:
  0.0 1.0 %copy-start = (bf16[4,64,8,128]{3,2,1,0:T(8,128)(2,1)S(1)}, bf16[4,64,8,128]{3,2,1,0:T(8,128)(2,1)}, u32[]{:S(2)}) copy-start(bf16[4,64,8,128]{3,2,1,0:T(8,128)(2,1)} %src.1) | copy-start | bytes 1572868
  1.3 17.2 %collective-permute-start.3 = (bf16[8,64,128]{2,1,0:T(8,128)(2,1)S(1)}, bf16[8,64,128]{2,1,0:T(8,128)(2,1)S(1)}, u32[]{:S(2)}, u32[]{:S(2)}) collective-permute-start(bf16[8,64,128]{2,1,0:T(8,128)(2,1)S(1)} %get-tuple-element.20), channel_id=1, source_target_pairs={{0,8},{1,9},{2,10},{3,11},{4,12},{5,13},{6,14},{7,15},{8,0},{9,1},... | collective-permute-start | bytes 393224 | tf_op jit(solution)/shard_map/ppermute | solution.py:180
  12.2 12.1 %collective-permute-start.4 = (bf16[8,64,128]{2,1,0:T(8,128)(2,1)S(1)}, bf16[8,64,128]{2,1,0:T(8,128)(2,1)S(1)}, u32[]{:S(2)}, u32[]{:S(2)}) collective-permute-start(bf16[8,64,128]{2,1,0:T(8,128)(2,1)S(1)} %get-tuple-element.21), channel_id=1, source_target_pairs={{0,12},{1,13},{2,14},{3,15},{4,8},{5,9},{6,10},{7,11},{8,4},{9,5},... | collective-permute-start | bytes 393224 | tf_op jit(solution)/shard_map/ppermute | solution.py:180
  14.2 18.5 %collective-permute-start = (bf16[8,64,128]{2,1,0:T(8,128)(2,1)S(1)}, bf16[8,64,128]{2,1,0:T(8,128)(2,1)S(1)}, u32[]{:S(2)}, u32[]{:S(2)}) collective-permute-start(bf16[8,64,128]{2,1,0:T(8,128)(2,1)S(1)} %get-tuple-element.17), channel_id=1, source_target_pairs={{0,4},{1,5},{2,6},{3,7},{4,0},{5,1},{6,2},{7,3},{8,12},{9,13},{10,... | collective-permute-start | bytes 393224 | tf_op jit(solution)/shard_map/ppermute | solution.py:180
  24.3 13.8 %copy-start.2 = (bf16[3,3,64,64]{3,2,1,0:T(8,128)(2,1)S(1)}, bf16[3,3,64,64]{3,2,1,0:T(8,128)(2,1)}, u32[]{:S(2)}) copy-start(bf16[3,3,64,64]{3,2,1,0:T(8,128)(2,1)} %param.7) | copy-start | bytes 221188
  24.3 13.8 %copy-start.1 = (bf16[3,3,64,128]{3,2,1,0:T(8,128)(2,1)S(1)}, bf16[3,3,64,128]{3,2,1,0:T(8,128)(2,1)}, u32[]{:S(2)}) copy-start(bf16[3,3,64,128]{3,2,1,0:T(8,128)(2,1)} %param.6) | copy-start | bytes 442372
  24.3 14.6 %collective-permute-start.5 = (bf16[4,128,128]{2,1,0:T(8,128)(2,1)S(1)}, bf16[4,128,128]{2,1,0:T(8,128)(2,1)S(1)}, u32[]{:S(2)}, u32[]{:S(2)}) collective-permute-start(bf16[4,128,128]{2,1,0:T(8,128)(2,1)S(1)} %get-tuple-element.22), channel_id=1, source_target_pairs={{0,16},{16,0},{32,48},{48,32},{64,80},{80,64},{96,112},{112,96},{1... | collective-permute-start | bytes 393224 | tf_op jit(solution)/shard_map/ppermute | solution.py:183
  26.4 12.5 %collective-permute-start.6 = (bf16[4,128,128]{2,1,0:T(8,128)(2,1)S(1)}, bf16[4,128,128]{2,1,0:T(8,128)(2,1)S(1)}, u32[]{:S(2)}, u32[]{:S(2)}) collective-permute-start(bf16[4,128,128]{2,1,0:T(8,128)(2,1)S(1)} %get-tuple-element.23), channel_id=1, source_target_pairs={{16,32},{32,16},{48,64},{64,48},{80,96},{96,80},{112,128},{128,112... | collective-permute-start | bytes 393224 | tf_op jit(solution)/shard_map/ppermute | solution.py:186
  32.8 6.2 %collective-permute-start.1 = (bf16[4,128,128]{2,1,0:T(8,128)(2,1)S(1)}, bf16[4,128,128]{2,1,0:T(8,128)(2,1)S(1)}, u32[]{:S(2)}, u32[]{:S(2)}) collective-permute-start(bf16[4,128,128]{2,1,0:T(8,128)(2,1)S(1)} %get-tuple-element.18), channel_id=1, source_target_pairs={{0,16},{16,0},{32,48},{48,32},{64,80},{80,64},{96,112},{112,96},{1... | collective-permute-start | bytes 393224 | tf_op jit(solution)/shard_map/ppermute | solution.py:183
  34.7 9.9 %collective-permute-start.2 = (bf16[4,128,128]{2,1,0:T(8,128)(2,1)S(1)}, bf16[4,128,128]{2,1,0:T(8,128)(2,1)S(1)}, u32[]{:S(2)}, u32[]{:S(2)}) collective-permute-start(bf16[4,128,128]{2,1,0:T(8,128)(2,1)S(1)} %get-tuple-element.19), channel_id=1, source_target_pairs={{16,32},{32,16},{48,64},{64,48},{80,96},{96,80},{112,128},{128,112... | collective-permute-start | bytes 393224 | tf_op jit(solution)/shard_map/ppermute | solution.py:186
  38.0 0.7 %copy-start.3 = (f32[64]{0:T(128)S(1)}, f32[64]{0:T(128)}, u32[]{:S(2)}) copy-start(f32[64]{0:T(128)} %param.8) | copy-start | bytes 772
  38.1 0.7 %copy-start.4 = (f32[64]{0:T(128)S(1)}, f32[64]{0:T(128)}, u32[]{:S(2)}) copy-start(f32[64]{0:T(128)} %param.9) | copy-start | bytes 772
